TPU v7x, 128 devices: a whole 4x4x4 slice. The times are simulated.
128 devices in a mesh: gy: 16 (over z, y), gz: 8 (over x, core).
Axes of the slice: x: 4, y: 4, z: 4, core: 2. Of those that a mesh axis runs over, the one named last changes fastest.
Arguments:
- eddy_cells: int32 [16, 8, 2, 2048], P('gy', 'gz'), may hold values from 0 to 32767, as said below
- eddy_signs: int32 [16, 8, 3, 2048], P('gy', 'gz'), may hold values from -1 to 1, as said below
- eddy_counts: int32 [16, 8], P('gy', 'gz'), may hold values from 256 to 2048
- stress_diag: float32 [3, 32768], P(None, 'gy'), may hold values from 0.3 to 3
- stress_shear: float32 [3, 32768], P(None, 'gy'), may hold values from -3 to 3
- mean_flow: float32 [3, 32768, 2048], P(None, 'gy', 'gz'), may hold values from -6 to 6
Outputs:
- velocity: float32 [3, 32768, 2048], P(None, 'gy', 'gz')
Inputs may be any that keep to these rules, and one draw needn't show every extreme that they name: `eddy_cells`: every slot of tile (i, j) holds a wall-normal cell in [i * 2048, (i + 1) * 2048) and a spanwise cell in [j * 256, (j + 1) * 256); only the first eddy_counts[i, j] slots are eddies. `eddy_signs`: each entry is -1 or 1.
All inputs are finite; a program needn't handle non-finite values.
Results may differ from a plain program's by a relative error of at most 0.0001.
Values sent between devices are 32-bit elements; how exact they have to be, the bound alone decides.
A program may use at most 128 MiB of HBM per device.

v0:
```python
import math

import jax
import jax.numpy as jnp
from jax import lax
from jax.sharding import Mesh
from jax.sharding import PartitionSpec as P

TY = 2048
TZ = 256
CAP = 2048
HALF = 128
GY_GZ = ("gy_0", "gy_1", "gz_0", "gz_1")
GY = ("gy_0", "gy_1")
GZ = ("gz_0", "gz_1")


shape_peak = math.sqrt(1.5)


def over_axes(value, axes):
    for axis in axes:
        value = lax.psum(value, axis)
    return value


def passed_along(value, axis, by):
    peers = lax.axis_size(axis)
    pairs = [(i, i + by) for i in range(peers) if 0 <= i + by < peers]
    return lax.ppermute(value, axis, pairs)


def passed_along_2(value, axis, by):
    peers = lax.axis_size(axis)
    return lax.ppermute(value, axis, [(i, (i + by) % peers) for i in range(peers)])


def profile(offsets):
    return shape_peak * jnp.maximum(1.0 - jnp.abs(offsets).astype(jnp.float32) / HALF, 0.0)


def tile_field(
    positions, signs_here, slot_low, slot_high, row_anchor, col_anchor, first_block, end_block
):
    block_size = min(256, CAP)
    ext_rows = TY + 2 * HALF
    ext_cols = TZ + 2 * HALF
    row_cells = row_anchor - HALF + jnp.arange(ext_rows, dtype=jnp.int32)
    col_cells = col_anchor - HALF + jnp.arange(ext_cols, dtype=jnp.int32)

    def add_block(block_index, running):
        first_slot = (block_index * block_size).astype(jnp.int32)
        slot_index = first_slot + jnp.arange(block_size, dtype=jnp.int32)
        places = lax.dynamic_slice_in_dim(positions, first_slot, block_size, 1)
        weights = lax.dynamic_slice_in_dim(signs_here, first_slot, block_size, 1).astype(
            jnp.float32
        )
        inside = jnp.logical_and(slot_index < slot_high, slot_index >= slot_low)
        weights = weights * inside.astype(jnp.float32)[None, :]
        wall_profile = profile(row_cells[:, None] - places[0][None, :])
        span_profile = profile(col_cells[:, None] - places[1][None, :])
        signed = (weights[:, None, :] * wall_profile[None, :, :]).reshape(3 * ext_rows, block_size)
        return running + lax.dot_general(
            signed,
            span_profile,
            (((1,), (1,)), ((), ())),
            precision=lax.Precision.HIGHEST,
            preferred_element_type=jnp.float32,
        )

    initial = jnp.zeros((3 * ext_rows, ext_cols), jnp.float32)
    return lax.fori_loop(first_block, end_block, add_block, initial).reshape(3, ext_rows, ext_cols)


def rescale(raw_field, stress_diag, stress_shear, mean_flow, amplitude):
    streamwise = stress_diag[0][:, None] * raw_field[0]
    normal_part = stress_shear[0][:, None] * raw_field[0] + stress_diag[1][:, None] * raw_field[1]
    spanwise = (
        stress_shear[1][:, None] * raw_field[0]
        + stress_shear[2][:, None] * raw_field[1]
        + stress_diag[2][:, None] * raw_field[2]
    )
    return mean_flow + amplitude * jnp.stack([streamwise, normal_part, spanwise])


def body(eddy_cells, eddy_signs, eddy_counts, stress_diag, stress_shear, mean_flow):
    live_count = eddy_counts.reshape(())
    eddy_total = over_axes(live_count.astype(jnp.float32), GY_GZ)
    positions = eddy_cells.reshape(2, CAP)
    signs_here = eddy_signs.reshape(3, CAP)
    block_size = min(256, CAP)
    row_anchor = lax.axis_index(GY) * TY
    col_anchor = lax.axis_index(GZ) * TZ
    zero_block = jnp.int32(0)
    block_count = (live_count + block_size - 1) // block_size
    extended = tile_field(
        positions,
        signs_here,
        zero_block,
        live_count,
        row_anchor,
        col_anchor,
        zero_block,
        block_count,
    )
    from_below = passed_along(extended[:, :HALF, :], GY, -1)
    from_above = passed_along(extended[:, TY + HALF :, :], GY, 1)
    rows_done = extended[:, HALF : HALF + TY, :]
    rows_done = rows_done.at[:, TY - HALF :, :].add(from_below)
    rows_done = rows_done.at[:, :HALF, :].add(from_above)
    from_right = passed_along_2(rows_done[:, :, :HALF], GZ, -1)
    from_left = passed_along_2(rows_done[:, :, TZ + HALF :], GZ, 1)
    interior = rows_done[:, :, HALF : HALF + TZ]
    interior = interior.at[:, :, TZ - HALF :].add(from_right)
    interior = interior.at[:, :, :HALF].add(from_left)
    amplitude = jnp.sqrt(
        TY * lax.axis_size(GY) * (TZ * lax.axis_size(GZ)) / (HALF * HALF) / eddy_total
    )
    return rescale(interior, stress_diag, stress_shear, mean_flow, amplitude)


def solution(mesh):
    split = Mesh(mesh.devices.reshape(4, 4, 4, 2), ("gy_0", "gy_1", "gz_0", "gz_1"))
    return jax.shard_map(
        body,
        mesh=split,
        in_specs=(
            P(GY, GZ, None, None),
            P(GY, GZ, None, None),
            P(GY, GZ),
            P(None, GY),
            P(None, GY),
            P(None, GY, GZ),
        ),
        out_specs=P(None, GY, GZ),
        check_vma=False,
    )
```

profile of v0, /device:TPU:1, one launch (start us, length us, event | category | flops | bytes accessed | tf_op | source)
XLA Modules:
  0.0 258.1 jit_solution(9215272168527139913)
XLA Ops:
  1.5 6.9 %broadcast_in_dim.2 = f32[6912,512]{1,0:T(8,128)} broadcast(f32[]{:T(128)} %constant.165.clone.1), dimensions={} | broadcast | bytes 14155780 | tf_op jit(solution)/shard_map/broadcast_in_dim | solution.py:71
  8.3 98.4 %while.15 = (s32[]{:T(128)}, f32[6912,512]{1,0:T(8,128)}, s32[]{:T(128)}, s32[3,2048]{1,0:T(4,128)S(1)}, s32[]{:T(128)}, /*index=5*/s32[2,2048]{1,0:T(2,128)}, s...) while((s32[]{:T(128)}, f32[6912,512]{1,0:T(8,128)}, ...), condition=%wide.region_5.6_spmd.clone, body=%wide.region_4.5_spmd.clone.sunk | while | flops 10881996800 | bytes 47226064 | solution.py:72
  9.0 0.8 fusion.38
  9.8 0.8 maximum_multiply_fusion.3
  11.2 16.8 %convolution_add_fusion.2 = f32[6912,512]{1,0:T(8,128)} fusion(f32[6912,512]{1,0:T(8,128)} %get-tuple-element.218, f32[6912,256]{1,0:T(8,128)S(1)} %bitcast.26, s32[256]{0:T(256)S(1)} %bitcast.32, s32[512]{0:T(512)S(1)} %iota_add_fusion.5), kind=kOutput, calls=%fused_computation.2.clone.1 | convolution fusion | flops 10876092416 | bytes 35392512 | tf_op jit(solution)/shard_map/while/body/dot_general | solution.py:63
  28.7 0.8 fusion.38
  29.5 0.8 maximum_multiply_fusion.3
  30.9 16.8 %convolution_add_fusion.2 = f32[6912,512]{1,0:T(8,128)} fusion(f32[6912,512]{1,0:T(8,128)} %get-tuple-element.218, f32[6912,256]{1,0:T(8,128)S(1)} %bitcast.26, s32[256]{0:T(256)S(1)} %bitcast.32, s32[512]{0:T(512)S(1)} %iota_add_fusion.5), kind=kOutput, calls=%fused_computation.2.clone.1 | convolution fusion | flops 10876092416 | bytes 35392512 | tf_op jit(solution)/shard_map/while/body/dot_general | solution.py:63
  48.3 0.8 fusion.38
  50.5 16.8 %convolution_add_fusion.2 = f32[6912,512]{1,0:T(8,128)} fusion(f32[6912,512]{1,0:T(8,128)} %get-tuple-element.218, f32[6912,256]{1,0:T(8,128)S(1)} %bitcast.26, s32[256]{0:T(256)S(1)} %bitcast.32, s32[512]{0:T(512)S(1)} %iota_add_fusion.5), kind=kOutput, calls=%fused_computation.2.clone.1 | convolution fusion | flops 10876092416 | bytes 35392512 | tf_op jit(solution)/shard_map/while/body/dot_general | solution.py:63
  68.0 0.8 fusion.38
  70.2 16.8 %convolution_add_fusion.2 = f32[6912,512]{1,0:T(8,128)} fusion(f32[6912,512]{1,0:T(8,128)} %get-tuple-element.218, f32[6912,256]{1,0:T(8,128)S(1)} %bitcast.26, s32[256]{0:T(256)S(1)} %bitcast.32, s32[512]{0:T(512)S(1)} %iota_add_fusion.5), kind=kOutput, calls=%fused_computation.2.clone.1 | convolution fusion | flops 10876092416 | bytes 35392512 | tf_op jit(solution)/shard_map/while/body/dot_general | solution.py:63
  87.7 0.8 fusion.38
  89.9 16.8 %convolution_add_fusion.2 = f32[6912,512]{1,0:T(8,128)} fusion(f32[6912,512]{1,0:T(8,128)} %get-tuple-element.218, f32[6912,256]{1,0:T(8,128)S(1)} %bitcast.26, s32[256]{0:T(256)S(1)} %bitcast.32, s32[512]{0:T(512)S(1)} %iota_add_fusion.5), kind=kOutput, calls=%fused_computation.2.clone.1 | convolution fusion | flops 10876092416 | bytes 35392512 | tf_op jit(solution)/shard_map/while/body/dot_general | solution.py:63
  106.7 1.5 fusion.28
  108.2 1.3 collective-permute-start
  109.5 24.4 %collective-permute-start.1 = (f32[3,128,512]{2,1,0:T(8,128)S(1)}, f32[3,128,512]{2,1,0:T(8,128)S(1)}, u32[]{:S(2)}, u32[]{:S(2)}) collective-permute-start(f32[3,128,512]{2,1,0:T(8,128)S(1)} %get-tuple-element.137), channel_id=1, source_target_pairs={{0,8},{8,16},{16,24},{24,32},{32,40},{40,48},{48,56},{56,64},{64,7... | collective-permute-start | bytes 2359304 | tf_op jit(solution)/shard_map/ppermute | solution.py:30
  133.9 10.7 %slice.194 = f32[3,2048,512]{2,1,0:T(8,128)} slice(f32[3,2304,512]{2,1,0:T(8,128)} %bitcast.28), slice={[0:3], [128:2176], [0:512]} | slice | bytes 25165824 | tf_op jit(solution)/shard_map/slice | solution.py:108
  144.6 2.2 fusion.26
  146.8 2.1 fusion.25
  148.9 4.9 %fusion.29 = (f32[3,2048,128]{2,1,0:T(8,128)S(1)}, f32[3,2048,128]{2,1,0:T(8,128)}) fusion(f32[3,2048,512]{2,1,0:T(8,128)} %fusion.25), kind=kLoop, calls=%fused_computation.44 | loop fusion | bytes 12582912 | tf_op jit(solution)/shard_map/slice | solution.py:112
  153.8 40.6 %collective-permute-start.2 = (f32[3,2048,128]{2,1,0:T(8,128)}, f32[3,2048,128]{2,1,0:T(8,128)}, u32[]{:S(2)}, u32[]{:S(2)}) collective-permute-start(f32[3,2048,128]{2,1,0:T(8,128)} %get-tuple-element.140), channel_id=1, source_target_pairs={{0,7},{1,0},{2,1},{3,2},{4,3},{5,4},{6,5},{7,6},{8,15},{9,8},{10,9... | collective-permute-start | bytes 9437192 | tf_op jit(solution)/shard_map/ppermute | solution.py:35
  194.5 5.8 %collective-permute-start.3 = (f32[3,2048,128]{2,1,0:T(8,128)S(1)}, f32[3,2048,128]{2,1,0:T(8,128)}, u32[]{:S(2)}, u32[]{:S(2)}) collective-permute-start(f32[3,2048,128]{2,1,0:T(8,128)S(1)} %get-tuple-element.139), channel_id=1, source_target_pairs={{0,1},{1,2},{2,3},{3,4},{4,5},{5,6},{6,7},{7,0},{8,9},{9,10},{10,1... | collective-permute-start | bytes 9437192 | tf_op jit(solution)/shard_map/ppermute | solution.py:35
  200.2 6.9 %psum.28 = f32[]{:T(128)} all-reduce(f32[]{:T(128)S(6)} %convert_element_type.23), channel_id=1, replica_groups=mesh['gy_0'=4,'gy_1'=4,'gz_0'=4,'gz_1'=2] {'gy_0'}, use_global_device_ids=true, to_apply=%region_0.0 | all-reduce | flops 1 | bytes 8 | tf_op jit(solution)/shard_map/psum | solution.py:23
  207.2 8.7 %psum.29 = f32[]{:T(128)} all-reduce(f32[]{:T(128)} %psum.28), channel_id=1, replica_groups=mesh['gy_0'=4,'gy_1'=4,'gz_0'=4,'gz_1'=2] {'gy_1'}, use_global_device_ids=true, to_apply=%region_1.0 | all-reduce | flops 1 | bytes 8 | tf_op jit(solution)/shard_map/psum | solution.py:23
  215.8 23.2 %psum.30 = f32[]{:T(128)} all-reduce(f32[]{:T(128)} %psum.29), channel_id=1, replica_groups=mesh['gy_0'=4,'gy_1'=4,'gz_0'=4,'gz_1'=2] {'gz_0'}, use_global_device_ids=true, to_apply=%region_2.0 | all-reduce | flops 1 | bytes 8 | tf_op jit(solution)/shard_map/psum | solution.py:23
  239.0 3.1 %psum.31 = f32[]{:T(128)} all-reduce(f32[]{:T(128)} %psum.30), channel_id=1, replica_groups=mesh['gy_0'=4,'gy_1'=4,'gz_0'=4,'gz_1'=2] {'gz_1'}, use_global_device_ids=true, to_apply=%region_3.0 | all-reduce | flops 1 | bytes 8 | tf_op jit(solution)/shard_map/psum | solution.py:23
  243.0 3.2 %slice.199 = f32[3,2048,256]{2,1,0:T(8,128)S(1)} slice(f32[3,2048,512]{2,1,0:T(8,128)} %fusion.25), slice={[0:3], [0:2048], [128:384]} | slice | bytes 12582912 | tf_op jit(solution)/shard_map/slice | solution.py:113
  246.2 3.2 %fusion.23 = f32[3,2048,256]{2,1,0:T(8,128)S(1)} fusion(f32[3,2048,256]{2,1,0:T(8,128)S(1)} %slice.199, f32[3,2048,128]{2,1,0:T(8,128)} %collective-permute-done.2, f32[3,2048,512]{2,1,0:T(8,128)} %fusion.25), kind=kLoop, calls=%fused_computation.32 | loop fusion | flops 786432 | bytes 9437184 | tf_op jit(solution)/shard_map/scatter-add | solution.py:114
  249.4 2.6 %fusion.22 = f32[3,2048,256]{2,1,0:T(8,128)S(1)} fusion(f32[3,2048,256]{2,1,0:T(8,128)S(1)} %fusion.23, f32[3,2048,128]{2,1,0:T(8,128)} %collective-permute-done.3), kind=kLoop, calls=%fused_computation.30 | loop fusion | flops 786432 | bytes 9437184 | tf_op jit(solution)/shard_map/scatter-add | solution.py:115
  252.0 2.1 slice_multiply_fusion.1
  254.9 3.2 %fusion.21 = f32[3,2048,256]{2,1,0:T(8,128)} fusion(f32[3,2048,256]{2,1,0:T(8,128)S(1)} %bitcast.31, f32[1,2048,256]{2,1,0:T(8,128)S(1)} %get-tuple-element.142, f32[1,2048,256]{2,1,0:T(8,128)S(1)} %get-tuple-element.143, f32[1,2048,256]{2,1,0:T(8,128)S(1)} %get-tuple-element.141, f32[]{:T(128)S(6)} %sqrt.3), kind=kLoop, calls=%fused_computation.28 | loop fusion | flops 6291456 | bytes 18874372 | tf_op jit(solution)/shard_map/add | solution.py:83
  (44 shorter events, 9.9 us)
Async XLA Ops:
  108.2 36.4 %collective-permute-start = (f32[3,128,512]{2,1,0:T(8,128)S(1)}, f32[3,128,512]{2,1,0:T(8,128)S(1)}, u32[]{:S(2)}, u32[]{:S(2)}) collective-permute-start(f32[3,128,512]{2,1,0:T(8,128)S(1)} %get-tuple-element.138), channel_id=1, source_target_pairs={{8,0},{16,8},{24,16},{32,24},{40,32},{48,40},{56,48},{64,56},{72,6... | collective-permute-start | bytes 2359304 | tf_op jit(solution)/shard_map/ppermute | solution.py:30
  109.5 37.3 %collective-permute-start.1 = (f32[3,128,512]{2,1,0:T(8,128)S(1)}, f32[3,128,512]{2,1,0:T(8,128)S(1)}, u32[]{:S(2)}, u32[]{:S(2)}) collective-permute-start(f32[3,128,512]{2,1,0:T(8,128)S(1)} %get-tuple-element.137), channel_id=1, source_target_pairs={{0,8},{8,16},{16,24},{24,32},{32,40},{40,48},{48,56},{56,64},{64,7... | collective-permute-start | bytes 2359304 | tf_op jit(solution)/shard_map/ppermute | solution.py:30
  148.9 94.0 %copy-start = (f32[3,2048]{1,0:T(4,128)S(1)}, f32[3,2048]{1,0:T(4,128)}, u32[]{:S(2)}) copy-start(f32[3,2048]{1,0:T(4,128)} %param.19) | copy-start | bytes 73732
  148.9 94.0 %copy-start.1 = (f32[3,2048]{1,0:T(4,128)S(1)}, f32[3,2048]{1,0:T(4,128)}, u32[]{:S(2)}) copy-start(f32[3,2048]{1,0:T(4,128)} %param.20) | copy-start | bytes 73732
  153.8 92.3 %collective-permute-start.2 = (f32[3,2048,128]{2,1,0:T(8,128)}, f32[3,2048,128]{2,1,0:T(8,128)}, u32[]{:S(2)}, u32[]{:S(2)}) collective-permute-start(f32[3,2048,128]{2,1,0:T(8,128)} %get-tuple-element.140), channel_id=1, source_target_pairs={{0,7},{1,0},{2,1},{3,2},{4,3},{5,4},{6,5},{7,6},{8,15},{9,8},{10,9... | collective-permute-start | bytes 9437192 | tf_op jit(solution)/shard_map/ppermute | solution.py:35
  194.5 54.9 %collective-permute-start.3 = (f32[3,2048,128]{2,1,0:T(8,128)S(1)}, f32[3,2048,128]{2,1,0:T(8,128)}, u32[]{:S(2)}, u32[]{:S(2)}) collective-permute-start(f32[3,2048,128]{2,1,0:T(8,128)S(1)} %get-tuple-element.139), channel_id=1, source_target_pairs={{0,1},{1,2},{2,3},{3,4},{4,5},{5,6},{6,7},{7,0},{8,9},{9,10},{10,1... | collective-permute-start | bytes 9437192 | tf_op jit(solution)/shard_map/ppermute | solution.py:35
  252.0 2.2 slice-start
  252.0 2.9 %slice-start.1 = ((s8[6291456]{0:T(1024)(128)(4,1)}), s8[2097152]{0:T(1024)(128)(4,1)S(1)}, s32[]{:S(2)}) async-start(s8[6291456]{0:T(1024)(128)(4,1)} %bitcast.30), calls=%async_computation.1 | async-start | bytes 4194304
where the time goes:
time: 257 us; the launch traced here: 258 us
  matrix products  84.1 us (33%)
  starting transfers between devices  72 us (28%)
  blocking collectives  42 us (16%)
  local copies, waits for them, and re-layouts  32.9 us (13%)
  other arithmetic  25.4 us (10%)
    dot_general x5, matrix products, add_block(): lax.dot_general(signed, span_profile, (((1,), (1,)), ((), ())), precision...  84.1 us
    ppermute x2, starting transfers between devices, passed_along_2(): lax.ppermute(value, axis, [(i, (i + by) % peers) for i in range(peers)])  46.4 us
    psum x4, blocking collectives, over_axes(): value = lax.psum(value, axis)  42 us
    ppermute x2, starting transfers between devices, passed_along(): return lax.ppermute(value, axis, pairs)  25.7 us
    slice x1, local copies, waits for them, and re-layouts, body(): rows_done = extended[:, HALF:HALF + TY, :]  10.7 us
    broadcast_in_dim x1, local copies, waits for them, and re-layouts, tile_field(): initial = jnp.zeros((3 * ext_rows, ext_cols), jnp.float32)  6.87 us
  transfers between devices with their start and end apart: 4, of which 0 were waited for; matrix products, arithmetic and copies ran while one was open for 7% of the time, Pallas kernels for 0%

commit v1 on v0

v1 whole, which is shorter than its diff:
```python
import jax
import jax.numpy as jnp
from jax import lax
from jax.experimental import pallas as pl
from jax.experimental.pallas import tpu as pltpu
from jax.sharding import PartitionSpec as P

TY = 2048
TZ = 256
CAP = 2048
HALF = 128
GY = 16
GZ = 8
ROWS = CAP // 128
BLOCK = 256
BLOCKS = TY // BLOCK
DEAD = 1 << 22
MESH = pl.DeviceIdType.MESH
OFFSETS = tuple((di, dj) for di in (-1, 0, 1) for dj in (-1, 0, 1))
OWN = 4


def sort_keys(vregs):
    lane = lax.broadcasted_iota(jnp.int32, (8, 128), 1)
    row = lax.broadcasted_iota(jnp.int32, (8, 128), 0)
    index = row * 128 + lane
    bits = CAP.bit_length() - 1
    for up in range(1, bits + 1):
        for step in range(up - 1, -1, -1):
            if step == 10:
                vregs = [
                    (jnp.minimum(low, high), jnp.maximum(low, high)) for low, high in vregs
                ]
                continue
            own_bit = lax.shift_right_logical(index, step) & 1
            lower = own_bit == 0
            axis, size, by = (1, 128, 1 << step) if step < 7 else (0, 8, 1 << (step - 7))
            sorted_lists = []
            for halves in vregs:
                done = []
                for half, x in enumerate(halves):
                    if up < 10:
                        take_min = ((lax.shift_right_logical(index, up) & 1) ^ own_bit) == 0
                    elif up == 10 and half == 1:
                        take_min = own_bit == 1
                    else:
                        take_min = lower
                    ahead = pltpu.roll(x, size - by, axis)
                    if 2 * by == size:
                        other = ahead
                    else:
                        other = jnp.where(lower, ahead, pltpu.roll(x, by, axis))
                    done.append(
                        jnp.where(take_min, jnp.minimum(x, other), jnp.maximum(x, other))
                    )
                sorted_lists.append(tuple(done))
            vregs = sorted_lists
    return vregs


def exchange(
    cells,
    signs,
    count,
    lists,
    bounds,
    total,
    places,
    stage,
    arrived,
    part1,
    got1,
    part2,
    got2,
    send_sem,
    recv_sem,
    send1,
    recv1,
    send2,
    recv2,
):
    gy = lax.axis_index("gy")
    gz = lax.axis_index("gz")
    barrier = pltpu.get_barrier_semaphore()

    def at(di, dj):
        return (lax.rem(gy + di + GY, GY), lax.rem(gz + dj + GZ, GZ))

    partners = [at(0, d) for d in range(1, GZ)] + [at(d, 0) for d in range(1, GY)]
    partners += [at(di, dj) for di, dj in OFFSETS if di and dj]
    for partner in partners:
        pl.semaphore_signal(barrier, inc=1, device_id=partner, device_id_type=MESH)

    live_count = count[0, 0]
    part1[...] = jnp.full((8, 128), live_count, jnp.int32).astype(jnp.float32)
    for r in range(ROWS):
        for k in range(2):
            places[k, r : r + 1, :] = cells[k : k + 1, 128 * r : 128 * r + 128]
    lane = lax.broadcasted_iota(jnp.int32, (8, 128), 1)
    row = lax.broadcasted_iota(jnp.int32, (8, 128), 0)
    keys = [[], [], []]
    for half in range(2):
        rows = slice(8 * half, 8 * half + 8)
        wall = places[0, rows, :] & (TY - 1)
        span = places[1, rows, :] & (TZ - 1)
        key = wall * 2048 + span * 8
        for c in range(3):
            key = key + lax.shift_right_logical(signs[c, rows, :] + 1, 1) * (1 << c)
        live = row * 128 + lane + 1024 * half < live_count
        key = jnp.where(live, key, DEAD)
        keys[0].append(key)
        keys[1].append(jnp.where(span < HALF - 1, key, DEAD))
        keys[2].append(jnp.where(span > HALF, key, DEAD))
    for kind, halves in enumerate(sort_keys([tuple(k) for k in keys])):
        for half, key in enumerate(halves):
            rows = slice(8 * half, 8 * half + 8)
            stage[kind, 0, rows, :] = lax.shift_right_logical(key, 11).astype(jnp.float32)
            stage[kind, 1, rows, :] = (lax.shift_right_logical(key, 3) & 255).astype(jnp.float32)
            live = key < DEAD
            for c in range(3):
                sign = (lax.shift_right_logical(key, c) & 1) * 2 - 1
                stage[kind, 2 + c, rows, :] = jnp.where(live, sign, 0).astype(jnp.float32)

    pl.semaphore_wait(barrier, len(partners))

    first = []
    for d in range(1, GZ):
        copy = pltpu.make_async_remote_copy(
            src_ref=part1,
            dst_ref=got1.at[d - 1],
            send_sem=send1.at[d - 1],
            recv_sem=recv1.at[d - 1],
            device_id=at(0, d),
            device_id_type=MESH,
        )
        copy.start()
        first.append(copy)
    sends = []
    for slot, (di, dj) in enumerate(OFFSETS):
        if di == 0 and dj == 0:
            continue
        copy = pltpu.make_async_remote_copy(
            src_ref=stage.at[{0: 0, 1: 1, -1: 2}[dj]],
            dst_ref=arrived.at[slot],
            send_sem=send_sem.at[slot],
            recv_sem=recv_sem.at[slot],
            device_id=at(-di, -dj),
            device_id_type=MESH,
        )
        copy.start()
        sends.append((slot, copy))
    for copy in first:
        copy.wait()
    mine = part1[...]
    for d in range(GZ - 1):
        mine = mine + got1[d]
    part2[...] = mine
    second = []
    for d in range(1, GY):
        copy = pltpu.make_async_remote_copy(
            src_ref=part2,
            dst_ref=got2.at[d - 1],
            send_sem=send2.at[d - 1],
            recv_sem=recv2.at[d - 1],
            device_id=at(d, 0),
            device_id_type=MESH,
        )
        copy.start()
        second.append(copy)

    lane16 = lax.broadcasted_iota(jnp.int32, (ROWS, 128), 1)

    def finish(slot, table):
        di, _ = OFFSETS[slot]
        lists[slot] = table[...]
        wall = table[0]
        starts = jnp.broadcast_to(wall[:, 0:1], (ROWS, 128))
        ends = jnp.broadcast_to(wall[:, 127:128], (ROWS, 128))
        low = (lane16 * BLOCK - (HALF - 1) - TY * di).astype(jnp.float32)
        high = jnp.minimum(
            (lane16 - BLOCKS) * BLOCK + (BLOCK + HALF - 2) - TY * di, TY - 1
        ).astype(jnp.float32)
        before = jnp.where(ends < low, 1.0, 0.0)
        begun = jnp.where(starts <= high, 1.0, 0.0)
        counted = jnp.sum(jnp.where(lane16 < BLOCKS, before, begun), axis=0, keepdims=True)
        if di:
            inside = jnp.logical_and(gy + di >= 0, gy + di < GY)
            counted = counted * jnp.where(inside, 1.0, 0.0)
        bounds[slot : slot + 1, :] = counted.astype(jnp.int32)

    finish(OWN, stage.at[0])
    for slot, copy in sends:
        copy.wait()
        finish(slot, arrived.at[slot])
    for copy in second:
        copy.wait()
    everything = part2[...]
    for d in range(GY - 1):
        everything = everything + got2[d]
    total[...] = everything


def tent(place, rows, first):
    bf = jnp.bfloat16
    y = (lax.broadcasted_iota(jnp.int32, (rows, 128), 0) + first).astype(jnp.float32).astype(bf)
    near = jnp.minimum(jnp.maximum(place, -256.0), 256.0).astype(bf)
    return jnp.maximum(bf(HALF) - jnp.abs(y - near), bf(0))


def evaluate(
    bounds, total, lists, diag, shear, mean, out, buffer, acc, scales, in_sem, out_sem
):
    def load(b):
        rows = pl.ds(pl.multiple_of(b * BLOCK, BLOCK), BLOCK)
        return pltpu.make_async_copy(mean.at[:, rows, :], buffer.at[:, rows, :], in_sem.at[b])

    def save(b):
        rows = pl.ds(pl.multiple_of(b * BLOCK, BLOCK), BLOCK)
        return pltpu.make_async_copy(buffer.at[:, rows, :], out.at[:, rows, :], out_sem.at[b])

    for b in range(BLOCKS):
        load(b).start()
    gain = jnp.sqrt(TY * GY * (TZ * GZ) / (HALF * HALF) / total[0:1, 0:1]) * (1.5 / (HALF * HALF))
    scales[0:3, :] = diag[...] * gain
    scales[3:6, :] = shear[...] * gain
    scales[6:8, :] = jnp.zeros((2, TY), jnp.float32)

    def add_list(slot, b):
        di, dj = OFFSETS[slot]
        begin, end = bounds[slot, b], bounds[slot, BLOCKS + b]
        anchor = (128 + b * BLOCK - TY * di).astype(jnp.float32)

        def pair(step, carry):
            r = begin + 2 * step
            left, right = [], []
            for part in range(2):
                chunk = r if part == 0 else jnp.minimum(r + 1, ROWS - 1)
                here = pl.ds(chunk, 1)
                left.append(tent(lists[slot, 0, here, :] - anchor, BLOCK, -128))
                q = lists[slot, 1, here, :] - 128.0 + TZ * dj
                if dj == 0:
                    shape = tent(q, TZ, -128)
                else:
                    shape = tent(q, HALF, -128 if dj < 0 else 0)
                signed = []
                for c in range(3):
                    s = lists[slot, 2 + c, here, :]
                    if part == 1:
                        s = s * jnp.where(r + 1 < ROWS, 1.0, 0.0)
                    signed.append(shape * s.astype(jnp.bfloat16))
                right.append(jnp.concatenate(signed, axis=0))
            product = lax.dot_general(
                jnp.concatenate(left, axis=1),
                jnp.concatenate(right, axis=1),
                (((1,), (1,)), ((), ())),
                preferred_element_type=jnp.float32,
            )
            if dj == 0:
                acc[...] += product
            else:
                for c in range(3):
                    at = c * TZ + (0 if dj < 0 else HALF)
                    acc[:, at : at + HALF] += product[:, c * HALF : (c + 1) * HALF]
            return carry

        lax.fori_loop(0, (end - begin + 1) // 2, pair, 0)

    @pl.loop(0, BLOCKS)
    def _(b):
        acc[...] = jnp.zeros_like(acc)
        for slot in (4, 3, 5):
            add_list(slot, b)

        @pl.when(b == 0)
        def _():
            for slot in (0, 1, 2):
                add_list(slot, b)

        @pl.when(b == BLOCKS - 1)
        def _():
            for slot in (6, 7, 8):
                add_list(slot, b)

        rows = pl.ds(pl.multiple_of(b * BLOCK, BLOCK), BLOCK)
        k = scales[:, rows].T
        raw = [acc[:, c * TZ : (c + 1) * TZ] for c in range(3)]
        load(b).wait()
        buffer[0, rows, :] += k[:, 0:1] * raw[0]
        buffer[1, rows, :] += k[:, 3:4] * raw[0] + k[:, 1:2] * raw[1]
        buffer[2, rows, :] += k[:, 4:5] * raw[0] + k[:, 5:6] * raw[1] + k[:, 2:3] * raw[2]
        save(b).start()

    for b in range(BLOCKS):
        save(b).wait()


def body(eddy_cells, eddy_signs, eddy_counts, stress_diag, stress_shear, mean_flow):
    vmem = pl.BlockSpec(memory_space=pltpu.VMEM)
    smem = pl.BlockSpec(memory_space=pltpu.SMEM)
    anywhere = pl.BlockSpec(memory_space=pl.ANY)
    dma = pltpu.SemaphoreType.DMA
    f32 = jnp.float32
    lists, bounds, total = pl.pallas_call(
        exchange,
        out_shape=(
            jax.ShapeDtypeStruct((9, 5, ROWS, 128), f32),
            jax.ShapeDtypeStruct((16, 128), jnp.int32),
            jax.ShapeDtypeStruct((8, 128), f32),
        ),
        in_specs=[vmem, vmem, smem],
        out_specs=(vmem, vmem, vmem),
        scratch_shapes=[
            pltpu.VMEM((2, ROWS, 128), jnp.int32),
            pltpu.VMEM((3, 5, ROWS, 128), f32),
            pltpu.VMEM((9, 5, ROWS, 128), f32),
            pltpu.VMEM((8, 128), f32),
            pltpu.VMEM((GZ - 1, 8, 128), f32),
            pltpu.VMEM((8, 128), f32),
            pltpu.VMEM((GY - 1, 8, 128), f32),
            dma((9,)),
            dma((9,)),
            dma((GZ - 1,)),
            dma((GZ - 1,)),
            dma((GY - 1,)),
            dma((GY - 1,)),
        ],
        compiler_params=pltpu.CompilerParams(collective_id=0, has_side_effects=True),
        name="exchange",
    )(
        eddy_cells.reshape(2, CAP),
        eddy_signs.reshape(3, ROWS, 128),
        eddy_counts,
    )
    return pl.pallas_call(
        evaluate,
        out_shape=jax.ShapeDtypeStruct((3, TY, TZ), f32),
        in_specs=[smem, vmem, vmem, vmem, vmem, anywhere],
        out_specs=anywhere,
        scratch_shapes=[
            pltpu.VMEM((3, TY, TZ), f32),
            pltpu.VMEM((BLOCK, 3 * TZ), f32),
            pltpu.VMEM((8, TY), f32),
            dma((BLOCKS,)),
            dma((BLOCKS,)),
        ],
        name="evaluate",
    )(bounds, total, lists, stress_diag, stress_shear, mean_flow)


def solution(mesh):
    return jax.shard_map(
        body,
        mesh=mesh,
        in_specs=(
            P("gy", "gz", None, None),
            P("gy", "gz", None, None),
            P("gy", "gz"),
            P(None, "gy"),
            P(None, "gy"),
            P(None, "gy", "gz"),
        ),
        out_specs=P(None, "gy", "gz"),
        check_vma=False,
    )
```

time: 257 us -> 39.8 us (0.15)
  matrix products: 84.1 us -> 0 us
  starting transfers between devices: 72 us -> 0 us
  blocking collectives: 42 us -> 0 us
  Pallas kernels: 0 us -> 39.1 us
  local copies, waits for them, and re-layouts: 32.9 us -> 0 us
  other arithmetic: 25.4 us -> 0 us
    dot_general x5 -> x0, matrix products: 84.1 us -> none  [add_block(): lax.dot_general(signed, span_profile, (((1,), (1,)), ((), ())), precision...]
    ppermute x4 -> x0, starting transfers between devices: 72 us -> none  [the longest x2 46.4 us: passed_along_2(): lax.ppermute(value, axis, [(i, (i + by) % peers) for i in range(peers)])]
    psum x4 -> x0, blocking collectives: 42 us -> none  [over_axes(): value = lax.psum(value, axis)]
    pallas_call x0 -> x2, Pallas kernels: none -> 39.1 us  [the longest x1 19.7 us: body(): pl.pallas_call(exchange, out_shape=(jax.ShapeDtypeStruct((9, 5, ROWS, 128...]
    slice x11 -> x0, local copies, waits for them, and re-layouts: 24.6 us -> none  [the longest x1 10.7 us: body(): rows_done = extended[:, HALF:HALF + TY, :]]
    scatter-add x4 -> x0, other arithmetic: 10.1 us -> none  [the longest x1 3.2 us: body(): interior = interior.at[:, :, TZ - HALF:].add(from_right)]
    mul x16 -> x0, other arithmetic: 8.74 us -> none  [the longest x5 3.77 us: profile(): shape_peak * jnp.maximum(1.0 - jnp.abs(offsets).astype(jnp.float32) / HAL...]
    broadcast_in_dim x1 -> x0, local copies, waits for them, and re-layouts: 6.87 us -> none  [tile_field(): initial = jnp.zeros((3 * ext_rows, ext_cols), jnp.float32)]
  transfers between devices with their start and end apart: 4 -> 0, of which waited for: 0 -> 0; matrix products, arithmetic and copies ran while one was open for 7% -> 0% of each run, Pallas kernels for 0% -> 0%
where the time goes in v1:
time: 39.8 us; the launch traced here: 39.7 us
  Pallas kernels  39.1 us (98%)
  between operations  0.66 us (2%)
    pallas_call x1, Pallas kernels, body(): pl.pallas_call(exchange, out_shape=(jax.ShapeDtypeStruct((9, 5, ROWS, 128...  19.7 us
    pallas_call x1, Pallas kernels, body(): pl.pallas_call(evaluate, out_shape=jax.ShapeDtypeStruct((3, TY, TZ), f32)...  19.4 us

profile of v1, /device:TPU:1, one launch (start us, length us, event | category | flops | bytes accessed | tf_op | source)
XLA Modules:
  0.0 39.7 jit_solution(5453057784745411474)
XLA Ops:
  0.7 19.7 %exchange.1 = (f32[9,5,16,128]{3,2,1,0:T(8,128)}, s32[16,128]{1,0:T(8,128)}, f32[8,128]{1,0:T(8,128)}) custom-call(s32[2,2048]{1,0:T(2,128)} %bitcast.3, s32[3,16,128]{2,1,0:T(8,128)} %bitcast.2, s32[1,1]{1,0:T(1,128)S(6)} %copy.7.count), custom_call_target="tpu_custom_call" | custom-call | tf_op jit(solution)/shard_map/exchange/pallas_call | solution.py:303
  20.3 19.4 %evaluate.1 = f32[3,2048,256]{2,1,0:T(8,128)} custom-call(s32[16,128]{1,0:T(8,128)} %get-tuple-element.8.bounds, f32[8,128]{1,0:T(8,128)} %get-tuple-element.9.total, f32[9,5,16,128]{3,2,1,0:T(8,128)} %get-tuple-element.10.lists, f32[3,2048]{1,0:T(4,128)} %diag.1, f32[3,2048]{1,0:T(4,128)} %shear.1, f32[3,2048,256]{2,1,0:T(8,128)} %mean.1), custom_call_target="tpu_custom_call" | custom-call | tf_op jit(solution)/shard_map/evaluate/pallas_call | solution.py:334

commit v2 on v1

--- a/solution.py
+++ b/solution.py
@@ -18,6 +18,7 @@
 MESH = pl.DeviceIdType.MESH
 OFFSETS = tuple((di, dj) for di in (-1, 0, 1) for dj in (-1, 0, 1))
 OWN = 4
+CHUNKS = {-1: 3, 0: 5, 1: 3}
 
 
 def sort_keys(vregs):
@@ -210,6 +211,8 @@
 def evaluate(
     bounds, total, lists, diag, shear, mean, out, buffer, acc, scales, in_sem, out_sem
 ):
+    bf = jnp.bfloat16
+
     def load(b):
         rows = pl.ds(pl.multiple_of(b * BLOCK, BLOCK), BLOCK)
         return pltpu.make_async_copy(mean.at[:, rows, :], buffer.at[:, rows, :], in_sem.at[b])
@@ -225,71 +228,107 @@
     scales[3:6, :] = shear[...] * gain
     scales[6:8, :] = jnp.zeros((2, TY), jnp.float32)
 
-    def add_list(slot, b):
-        di, dj = OFFSETS[slot]
-        begin, end = bounds[slot, b], bounds[slot, BLOCKS + b]
-        anchor = (128 + b * BLOCK - TY * di).astype(jnp.float32)
-
-        def pair(step, carry):
-            r = begin + 2 * step
-            left, right = [], []
-            for part in range(2):
-                chunk = r if part == 0 else jnp.minimum(r + 1, ROWS - 1)
-                here = pl.ds(chunk, 1)
-                left.append(tent(lists[slot, 0, here, :] - anchor, BLOCK, -128))
-                q = lists[slot, 1, here, :] - 128.0 + TZ * dj
+    def chunk_counts(dj, b):
+        slots = [(di + 1) * 3 + dj + 1 for di in (-1, 0, 1)]
+        begins = [bounds[slot, b] for slot in slots]
+        numbers = [
+            jnp.maximum(bounds[slot, BLOCKS + b] - begin, 0) for slot, begin in zip(slots, begins)
+        ]
+        return begins, numbers
+
+    def product(dj, b, begins, numbers, start, chunks):
+        left, right = [], []
+        above = numbers[0]
+        beside = above + numbers[1]
+        every = beside + numbers[2]
+        for part in range(chunks):
+            i = start + part
+            di = jnp.where(i < above, 0, jnp.where(i < beside, 1, 2))
+            base = jnp.where(
+                i < above,
+                begins[0],
+                jnp.where(i < beside, begins[1] - above, begins[2] - beside),
+            )
+            used = i < every
+            slot = jnp.where(used, di * 3 + dj + 1, 0)
+            chunk = pl.ds(jnp.where(used, base + i, 0), 1)
+            live = jnp.where(used, 1.0, 0.0)
+            anchor = (128 + b * BLOCK - TY * (di - 1)).astype(jnp.float32)
+            left.append(tent(lists[slot, 0, chunk, :] - anchor, BLOCK, -128))
+            q = lists[slot, 1, chunk, :] - 128.0 + TZ * dj
+            if dj == 0:
+                shape = tent(q, TZ, -128)
+            else:
+                shape = tent(q, HALF, -128 if dj < 0 else 0)
+            right.append(
+                jnp.concatenate(
+                    [shape * (lists[slot, 2 + c, chunk, :] * live).astype(bf) for c in range(3)],
+                    axis=0,
+                )
+            )
+        return lax.dot_general(
+            jnp.concatenate(left, axis=1),
+            jnp.concatenate(right, axis=1),
+            (((1,), (1,)), ((), ())),
+            preferred_element_type=jnp.float32,
+        )
+
+    def accumulate(b, side):
+        ranges = {dj: chunk_counts(dj, b) for dj in (-1, 0, 1)}
+        parts = {dj: product(dj, b, *ranges[dj], 0, CHUNKS[dj]) for dj in (-1, 0, 1)}
+        for c in range(3):
+            for half, dj in ((0, -1), (1, 1)):
+                at = c * TZ + half * HALF
+                acc[side, :, at : at + HALF] = (
+                    parts[0][:, at : at + HALF] + parts[dj][:, c * HALF : (c + 1) * HALF]
+                )
+        return ranges
+
+    def overflow(b, side, ranges):
+        for dj in (-1, 0, 1):
+            begins, numbers = ranges[dj]
+            chunks = CHUNKS[dj]
+
+            def more(step, carry, dj=dj, begins=begins, numbers=numbers, chunks=chunks):
+                extra = product(dj, b, begins, numbers, step * chunks, chunks)
                 if dj == 0:
-                    shape = tent(q, TZ, -128)
+                    acc[side] += extra
                 else:
-                    shape = tent(q, HALF, -128 if dj < 0 else 0)
-                signed = []
-                for c in range(3):
-                    s = lists[slot, 2 + c, here, :]
-                    if part == 1:
-                        s = s * jnp.where(r + 1 < ROWS, 1.0, 0.0)
-                    signed.append(shape * s.astype(jnp.bfloat16))
-                right.append(jnp.concatenate(signed, axis=0))
-            product = lax.dot_general(
-                jnp.concatenate(left, axis=1),
-                jnp.concatenate(right, axis=1),
-                (((1,), (1,)), ((), ())),
-                preferred_element_type=jnp.float32,
-            )
-            if dj == 0:
-                acc[...] += product
-            else:
-                for c in range(3):
-                    at = c * TZ + (0 if dj < 0 else HALF)
-                    acc[:, at : at + HALF] += product[:, c * HALF : (c + 1) * HALF]
-            return carry
-
-        lax.fori_loop(0, (end - begin + 1) // 2, pair, 0)
-
-    @pl.loop(0, BLOCKS)
-    def _(b):
-        acc[...] = jnp.zeros_like(acc)
-        for slot in (4, 3, 5):
-            add_list(slot, b)
-
-        @pl.when(b == 0)
-        def _():
-            for slot in (0, 1, 2):
-                add_list(slot, b)
-
-        @pl.when(b == BLOCKS - 1)
-        def _():
-            for slot in (6, 7, 8):
-                add_list(slot, b)
-
+                    for c in range(3):
+                        at = c * TZ + (0 if dj < 0 else HALF)
+                        acc[side, :, at : at + HALF] += extra[:, c * HALF : (c + 1) * HALF]
+                return carry
+
+            count = numbers[0] + numbers[1] + numbers[2]
+            lax.fori_loop(1, (count + chunks - 1) // chunks, more, 0)
+
+    def finish(b, side):
         rows = pl.ds(pl.multiple_of(b * BLOCK, BLOCK), BLOCK)
         k = scales[:, rows].T
-        raw = [acc[:, c * TZ : (c + 1) * TZ] for c in range(3)]
-        load(b).wait()
+        raw = [acc[side, :, c * TZ : (c + 1) * TZ] for c in range(3)]
         buffer[0, rows, :] += k[:, 0:1] * raw[0]
         buffer[1, rows, :] += k[:, 3:4] * raw[0] + k[:, 1:2] * raw[1]
         buffer[2, rows, :] += k[:, 4:5] * raw[0] + k[:, 5:6] * raw[1] + k[:, 2:3] * raw[2]
         save(b).start()
 
+    overflow(jnp.int32(0), 0, accumulate(jnp.int32(0), 0))
+
+    @pl.loop(0, BLOCKS // 2 - 1)
+    def _(twice):
+        for side in (1, 0):
+            b = 2 * twice + 2 - side
+            load(b - 1).wait()
+            ranges = accumulate(b, side)
+            finish(b - 1, 1 - side)
+            overflow(b, side, ranges)
+
+    b = jnp.int32(BLOCKS - 1)
+    load(b - 1).wait()
+    ranges = accumulate(b, 1)
+    finish(b - 1, 0)
+    overflow(b, 1, ranges)
+    load(b).wait()
+    finish(b, 1)
     for b in range(BLOCKS):
         save(b).wait()
 
@@ -331,6 +370,15 @@
         eddy_signs.reshape(3, ROWS, 128),
         eddy_counts,
     )
+    return call_evaluate(bounds, total, lists, stress_diag, stress_shear, mean_flow)
+
+
+def call_evaluate(bounds, total, lists, stress_diag, stress_shear, mean_flow):
+    vmem = pl.BlockSpec(memory_space=pltpu.VMEM)
+    smem = pl.BlockSpec(memory_space=pltpu.SMEM)
+    anywhere = pl.BlockSpec(memory_space=pl.ANY)
+    dma = pltpu.SemaphoreType.DMA
+    f32 = jnp.float32
     return pl.pallas_call(
         evaluate,
         out_shape=jax.ShapeDtypeStruct((3, TY, TZ), f32),
@@ -338,7 +386,7 @@
         out_specs=anywhere,
         scratch_shapes=[
             pltpu.VMEM((3, TY, TZ), f32),
-            pltpu.VMEM((BLOCK, 3 * TZ), f32),
+            pltpu.VMEM((2, BLOCK, 3 * TZ), f32),
             pltpu.VMEM((8, TY), f32),
             dma((BLOCKS,)),
             dma((BLOCKS,)),

time: 39.8 us -> 30.9 us (0.78)
  Pallas kernels: 39.1 us -> 30 us
    pallas_call x1, Pallas kernels: 19.4 us -> 10.4 us  [call_evaluate(): pl.pallas_call(evaluate, out_shape=jax.ShapeDtypeStruct((3, TY, TZ), f32)...]
where the time goes in v2:
time: 30.9 us; the launch traced here: 30.7 us
  Pallas kernels  30 us (97%)
  between operations  0.66 us (2%)
    pallas_call x1, Pallas kernels, body(): pl.pallas_call(exchange, out_shape=(jax.ShapeDtypeStruct((9, 5, ROWS, 128...  19.7 us
    pallas_call x1, Pallas kernels, call_evaluate(): pl.pallas_call(evaluate, out_shape=jax.ShapeDtypeStruct((3, TY, TZ), f32)...  10.4 us

profile of v2, /device:TPU:1, one launch (start us, length us, event | category | flops | bytes accessed | tf_op | source)
XLA Modules:
  0.0 30.7 jit_solution(6191146468909760537)
XLA Ops:
  0.7 19.7 %exchange.1 = (f32[9,5,16,128]{3,2,1,0:T(8,128)}, s32[16,128]{1,0:T(8,128)}, f32[8,128]{1,0:T(8,128)}) custom-call(s32[2,2048]{1,0:T(2,128)} %bitcast.3, s32[3,16,128]{2,1,0:T(8,128)} %bitcast.2, s32[1,1]{1,0:T(1,128)S(6)} %copy.7.count), custom_call_target="tpu_custom_call" | custom-call | tf_op jit(solution)/shard_map/exchange/pallas_call | solution.py:342
  20.3 10.4 %evaluate.1 = f32[3,2048,256]{2,1,0:T(8,128)} custom-call(s32[16,128]{1,0:T(8,128)} %get-tuple-element.8.bounds, f32[8,128]{1,0:T(8,128)} %get-tuple-element.9.total, f32[9,5,16,128]{3,2,1,0:T(8,128)} %get-tuple-element.10.lists, f32[3,2048]{1,0:T(4,128)} %diag.1, f32[3,2048]{1,0:T(4,128)} %shear.1, f32[3,2048,256]{2,1,0:T(8,128)} %mean.1), custom_call_target="tpu_custom_call" | custom-call | tf_op jit(solution)/shard_map/evaluate/pallas_call | solution.py:382

commit v3 on v1

v3 whole, which is shorter than its diff:
```python
import jax
import jax.numpy as jnp
from jax import lax
from jax.experimental import pallas as pl
from jax.experimental.pallas import tpu as pltpu
from jax.sharding import PartitionSpec as P

TY = 2048
TZ = 256
CAP = 2048
HALF = 128
GY = 16
GZ = 8
ROWS = CAP // 128
BLOCK = 256
BLOCKS = TY // BLOCK
DEAD = 1 << 22
VMEM_LIMIT = 36 << 20
MESH = pl.DeviceIdType.MESH
OFFSETS = tuple((di, dj) for di in (-1, 0, 1) for dj in (-1, 0, 1))
OWN = 4
SPLIT = 8
OWN_CHUNKS = 5
SIDE_CHUNKS = 3
END_CHUNKS = 2


def sort_keys(vregs):
    lane = lax.broadcasted_iota(jnp.int32, (8, 128), 1)
    row = lax.broadcasted_iota(jnp.int32, (8, 128), 0)
    index = row * 128 + lane
    bits = CAP.bit_length() - 1
    for up in range(1, bits + 1):
        for step in range(up - 1, -1, -1):
            if step == 10:
                vregs = [
                    (jnp.minimum(low, high), jnp.maximum(low, high)) for low, high in vregs
                ]
                continue
            own_bit = lax.shift_right_logical(index, step) & 1
            lower = own_bit == 0
            axis, size, by = (1, 128, 1 << step) if step < 7 else (0, 8, 1 << (step - 7))
            sorted_lists = []
            for halves in vregs:
                done = []
                for half, x in enumerate(halves):
                    if up < 10:
                        take_min = ((lax.shift_right_logical(index, up) & 1) ^ own_bit) == 0
                    elif up == 10 and half == 1:
                        take_min = own_bit == 1
                    else:
                        take_min = lower
                    ahead = pltpu.roll(x, size - by, axis)
                    if 2 * by == size:
                        other = ahead
                    else:
                        other = jnp.where(lower, ahead, pltpu.roll(x, by, axis))
                    done.append(
                        jnp.where(take_min, jnp.minimum(x, other), jnp.maximum(x, other))
                    )
                sorted_lists.append(tuple(done))
            vregs = sorted_lists
    return vregs


def exchange(
    cells_in,
    signs_in,
    count,
    mean,
    lists,
    bounds,
    total,
    own,
    held,
    places,
    stage,
    own_edges,
    own_bounds,
    list_bounds,
    bound_sem,
    arrived,
    part1,
    got1,
    part2,
    got2,
    send_sem,
    recv_sem,
    send1,
    recv1,
    send2,
    recv2,
    part3,
    got3,
    send3,
    recv3,
    mean_sem,
    cells,
    signs,
    input_sem,
):
    inputs = [
        pltpu.make_async_copy(cells_in, cells, input_sem.at[0]),
        pltpu.make_async_copy(signs_in, signs, input_sem.at[1]),
    ]
    for copy in inputs:
        copy.start()
    fetch = pltpu.make_async_copy(mean, held, mean_sem)
    fetch.start()
    gy = lax.axis_index("gy")
    gz = lax.axis_index("gz")
    barrier = pltpu.get_barrier_semaphore()

    def at(di, dj):
        return (lax.rem(gy + di + GY, GY), lax.rem(gz + dj + GZ, GZ))

    def along_y(d):
        return (gy - lax.rem(gy, 4) + lax.rem(gy + d, 4), gz)

    groups = [
        [at(0, d) for d in range(1, GZ)],
        [along_y(d) for d in range(1, 4)],
        [at(4 * d, 0) for d in range(1, 4)],
    ]
    for group in groups:
        for partner in group:
            pl.semaphore_signal(barrier, inc=1, device_id=partner, device_id_type=MESH)
    inside = {di: jnp.logical_and(gy + di >= 0, gy + di < GY) for di in (-1, 1)}
    for di in (-1, 1):

        @pl.when(inside[di])
        def _():
            for dj in (-1, 0, 1):
                pl.semaphore_signal(
                    barrier, inc=1, device_id=at(di, dj), device_id_type=MESH
                )

    live_count = count[0, 0]
    part1[...] = jnp.full((8, 128), live_count, jnp.int32).astype(jnp.float32)
    arrivals = sum(len(group) for group in groups)
    for di in (-1, 1):
        arrivals = arrivals + jnp.where(inside[di], 3, 0)
    pl.semaphore_wait(barrier, arrivals)

    def start_phase(phase):
        part, got, sent, received = phases[phase]
        copies = []
        for k, partner in enumerate(groups[phase]):
            copy = pltpu.make_async_remote_copy(
                src_ref=part,
                dst_ref=got.at[k],
                send_sem=sent.at[k],
                recv_sem=received.at[k],
                device_id=partner,
                device_id_type=MESH,
            )
            copy.start()
            copies.append(copy)
        return copies

    def end_phase(phase, copies, result):
        part, got, _, _ = phases[phase]
        for copy in copies:
            copy.wait()
        value = part[...]
        for k in range(len(copies)):
            value = value + got[k]
        result[...] = value

    phases = [
        (part1, got1, send1, recv1),
        (part2, got2, send2, recv2),
        (part3, got3, send3, recv3),
    ]
    counting = start_phase(0)

    for copy in inputs:
        copy.wait()
    for r in range(ROWS):
        for k in range(2):
            places[k, r : r + 1, :] = cells[k : k + 1, 128 * r : 128 * r + 128]
    lane = lax.broadcasted_iota(jnp.int32, (8, 128), 1)
    row = lax.broadcasted_iota(jnp.int32, (8, 128), 0)
    keys = [[], [], []]
    for half in range(2):
        rows = slice(8 * half, 8 * half + 8)
        wall = places[0, rows, :] & (TY - 1)
        span = places[1, rows, :] & (TZ - 1)
        key = wall * 2048 + span * 8
        for c in range(3):
            key = key + lax.shift_right_logical(signs[c, rows, :] + 1, 1) * (1 << c)
        live = row * 128 + lane + 1024 * half < live_count
        key = jnp.where(live, key, DEAD)
        keys[0].append(key)
        keys[1].append(jnp.where(span < HALF - 1, key, DEAD))
        keys[2].append(jnp.where(span > HALF, key, DEAD))
    for kind, halves in enumerate(sort_keys([tuple(k) for k in keys])):
        for half, key in enumerate(halves):
            rows = slice(8 * half, 8 * half + 8)
            stage[kind, 0, rows, :] = lax.shift_right_logical(key, 11)
            stage[kind, 1, rows, :] = lax.shift_right_logical(key, 3) & 255
            live = key < DEAD
            for c in range(3):
                sign = (lax.shift_right_logical(key, c) & 1) * 2 - 1
                stage[kind, 2 + c, rows, :] = jnp.where(live, sign, 0)

    sends = {}
    for slot, (di, dj) in enumerate(OFFSETS):
        if slot == OWN:
            continue
        sends[slot] = pltpu.make_async_remote_copy(
            src_ref=stage.at[{0: 0, 1: 1, -1: 2}[dj]],
            dst_ref=arrived.at[slot],
            send_sem=send_sem.at[slot],
            recv_sem=recv_sem.at[slot],
            device_id=at(-di, -dj),
            device_id_type=MESH,
        )
    for dj in (-1, 1):
        sends[4 + dj].start()
    for di in (-1, 1):

        @pl.when(inside[-di])
        def _():
            for dj in (-1, 0, 1):
                sends[4 + 3 * di + dj].start()

    lane16 = lax.broadcasted_iota(jnp.int32, (ROWS, 128), 1)

    def edges(slot, table):
        di, _ = OFFSETS[slot]
        wall = table[0]
        starts = jnp.broadcast_to(wall[:, 0:1], (ROWS, 128))
        ends = jnp.broadcast_to(wall[:, 127:128], (ROWS, 128))
        low = lane16 * BLOCK - (HALF - 1) - TY * di
        high = jnp.minimum(
            (lane16 - BLOCKS) * BLOCK + (BLOCK + HALF - 2) - TY * di, TY - 1
        )
        before = jnp.where(ends < low, 1, 0)
        begun = jnp.where(starts <= high, 1, 0)
        return jnp.sum(jnp.where(lane16 < BLOCKS, before, begun), axis=0, keepdims=True)

    own_edges[...] = jnp.broadcast_to(edges(OWN, stage.at[0]), (8, 128))
    lists[OWN] = stage[0]
    to_scalars = pltpu.make_async_copy(own_edges, own_bounds, bound_sem.at[0])
    to_scalars.start()
    end_phase(0, counting, part2)
    counting = start_phase(1)
    to_scalars.wait()

    def own_block(b):
        begin = own_bounds[0, b]
        number = jnp.maximum(own_bounds[0, BLOCKS + b] - begin, 0)
        own[b] = product(lists, 0, b, [0, begin, 0], [0, number, 0], 0, OWN_CHUNKS)

    pl.loop(0, SPLIT)(own_block)
    end_phase(1, counting, part3)
    counting = start_phase(2)
    pl.loop(SPLIT, BLOCKS)(own_block)

    bounds[OWN : OWN + 1, :] = own_edges[0:1, :]

    def finish(slot):
        lists[slot] = arrived[slot]
        bounds[slot : slot + 1, :] = edges(slot, arrived.at[slot])

    for dj in (-1, 1):
        sends[4 + dj].wait()
        finish(4 + dj)
    for di in (-1, 1):

        @pl.when(inside[-di])
        def _():
            for dj in (-1, 0, 1):
                sends[4 + 3 * di + dj].wait_send()

        @pl.when(inside[di])
        def _():
            for dj in (-1, 0, 1):
                slot = 4 + 3 * di + dj
                sends[slot].wait_recv()
                finish(slot)

        @pl.when(jnp.logical_not(inside[di]))
        def _():
            for dj in (-1, 0, 1):
                slot = 4 + 3 * di + dj
                lists[slot] = jnp.zeros((5, ROWS, 128), jnp.int32)
                bounds[slot : slot + 1, :] = jnp.zeros((1, 128), jnp.int32)

    bounds[9:16, :] = jnp.zeros((7, 128), jnp.int32)
    to_scalars = pltpu.make_async_copy(bounds, list_bounds, bound_sem.at[1])
    to_scalars.start()
    to_scalars.wait()

    def side_block(b):
        parts = {
            dj: product(lists, dj, b, *chunk_counts(list_bounds, dj, b), 0, SIDE_CHUNKS)
            for dj in (-1, 1)
        }
        for c in range(3):
            for half, dj in ((0, -1), (1, 1)):
                at = c * TZ + half * HALF
                own[b, :, at : at + HALF] += parts[dj][:, c * HALF : (c + 1) * HALF]

    pl.loop(0, BLOCKS)(side_block)
    for b in (0, BLOCKS - 1):
        ranges = chunk_counts(list_bounds, 0, b)
        own[b] += product(lists, 0, jnp.int32(b), *ranges, 0, END_CHUNKS)
    end_phase(2, counting, total)
    fetch.wait()


def chunk_counts(bounds, dj, b):
    slots = [(di + 1) * 3 + dj + 1 for di in (-1, 0, 1)]
    begins = [bounds[slot, b] for slot in slots]
    numbers = [
        jnp.maximum(bounds[slot, BLOCKS + b] - begin, 0) for slot, begin in zip(slots, begins)
    ]
    if dj == 0:
        begins[1] = numbers[1] = 0
    return begins, numbers


def product(lists, dj, b, begins, numbers, start, chunks):
    bf = jnp.bfloat16
    left, right = [], []
    above = numbers[0]
    beside = above + numbers[1]
    every = beside + numbers[2]
    for part in range(chunks):
        i = start + part
        di = jnp.where(i < above, 0, jnp.where(i < beside, 1, 2))
        base = jnp.where(
            i < above,
            begins[0],
            jnp.where(i < beside, begins[1] - above, begins[2] - beside),
        )
        used = i < every
        slot = jnp.where(used, di * 3 + dj + 1, OWN)
        chunk = pl.ds(jnp.where(used, base + i, 0), 1)
        live = jnp.where(used, 1, 0)
        anchor = 128 + b * BLOCK - TY * (di - 1)
        left.append(tent(lists[slot, 0, chunk, :] - anchor, BLOCK, -128))
        q = lists[slot, 1, chunk, :] - 128 + TZ * dj
        if dj == 0:
            shape = tent(q, TZ, -128)
        else:
            shape = tent(q, HALF, -128 if dj < 0 else 0)
        signed = [
            shape * (lists[slot, 2 + c, chunk, :] * live).astype(jnp.float32).astype(bf)
            for c in range(3)
        ]
        right.append(jnp.concatenate(signed, axis=0))
    return lax.dot_general(
        jnp.concatenate(left, axis=1),
        jnp.concatenate(right, axis=1),
        (((1,), (1,)), ((), ())),
        preferred_element_type=jnp.float32,
    )


def tent(place, rows, first):
    bf = jnp.bfloat16
    y = (lax.broadcasted_iota(jnp.int32, (rows, 128), 0) + first).astype(jnp.float32).astype(bf)
    near = jnp.minimum(jnp.maximum(place, -256), 256).astype(jnp.float32).astype(bf)
    return jnp.maximum(bf(HALF) - jnp.abs(y - near), bf(0))


def evaluate(bounds, total, lists, diag, shear, own, mean, out, buffer, acc, scales, out_sem):
    def save(b):
        rows = pl.ds(pl.multiple_of(b * BLOCK, BLOCK), BLOCK)
        return pltpu.make_async_copy(buffer.at[:, rows, :], out.at[:, rows, :], out_sem.at[b])

    gain = jnp.sqrt(TY * GY * (TZ * GZ) / (HALF * HALF) / total[0:1, 0:1]) * (1.5 / (HALF * HALF))
    scales[0:3, :] = diag[...] * gain
    scales[3:6, :] = shear[...] * gain
    scales[6:8, :] = jnp.zeros((2, TY), jnp.float32)

    def finish(b, raw):
        rows = pl.ds(pl.multiple_of(b * BLOCK, BLOCK), BLOCK)
        k = scales[:, rows].T
        raw = [raw[:, c * TZ : (c + 1) * TZ] for c in range(3)]
        buffer[0, rows, :] = mean[0, rows, :] + k[:, 0:1] * raw[0]
        buffer[1, rows, :] = mean[1, rows, :] + k[:, 3:4] * raw[0] + k[:, 1:2] * raw[1]
        buffer[2, rows, :] = (
            mean[2, rows, :] + k[:, 4:5] * raw[0] + k[:, 5:6] * raw[1] + k[:, 2:3] * raw[2]
        )
        save(b).start()

    def leftovers(b):
        begin = bounds[OWN, b]
        number = jnp.maximum(bounds[OWN, BLOCKS + b] - begin, 0)
        jobs = [(0, [0, begin, 0], [0, number, 0], OWN_CHUNKS)]
        for dj, done in ((-1, SIDE_CHUNKS), (0, END_CHUNKS), (1, SIDE_CHUNKS)):
            jobs.append((dj, *chunk_counts(bounds, dj, b), done))
        return jobs

    @pl.loop(0, BLOCKS)
    def _(b):
        jobs = leftovers(b)
        counts = [numbers[0] + numbers[1] + numbers[2] for _, _, numbers, _ in jobs]
        some = counts[0] > jobs[0][3]
        for count, job in zip(counts[1:], jobs[1:]):
            some = jnp.logical_or(some, count > job[3])

        @pl.when(some)
        def _():
            acc[...] = own[b]
            for count, (dj, begins, numbers, done) in zip(counts, jobs):

                def more(step, carry, dj=dj, begins=begins, numbers=numbers, done=done):
                    extra = product(lists, dj, b, begins, numbers, done + step * 2, 2)
                    if dj == 0:
                        acc[...] += extra
                    else:
                        for c in range(3):
                            at = c * TZ + (0 if dj < 0 else HALF)
                            acc[:, at : at + HALF] += extra[:, c * HALF : (c + 1) * HALF]
                    return carry

                lax.fori_loop(0, jnp.maximum(count - done + 1, 0) // 2, more, 0)
            finish(b, acc)

        @pl.when(jnp.logical_not(some))
        def _():
            finish(b, own.at[b])

    for b in range(BLOCKS):
        save(b).wait()


def body(eddy_cells, eddy_signs, eddy_counts, stress_diag, stress_shear, mean_flow):
    vmem = pl.BlockSpec(memory_space=pltpu.VMEM)
    smem = pl.BlockSpec(memory_space=pltpu.SMEM)
    anywhere = pl.BlockSpec(memory_space=pl.ANY)
    hbm = pl.BlockSpec(memory_space=pltpu.HBM)
    dma = pltpu.SemaphoreType.DMA
    f32, i32 = jnp.float32, jnp.int32
    lists, bounds, total, own, held = pl.pallas_call(
        exchange,
        out_shape=(
            pltpu.VMEM((9, 5, ROWS, 128), i32),
            jax.ShapeDtypeStruct((16, 128), jnp.int32),
            pltpu.VMEM((8, 128), f32),
            pltpu.VMEM((BLOCKS, BLOCK, 3 * TZ), f32),
            pltpu.VMEM((3, TY, TZ), f32),
        ),
        in_specs=[hbm, hbm, smem, hbm],
        out_specs=(vmem, vmem, vmem, vmem, vmem),
        scratch_shapes=[
            pltpu.VMEM((2, ROWS, 128), jnp.int32),
            pltpu.VMEM((3, 5, ROWS, 128), i32),
            pltpu.VMEM((8, 128), i32),
            pltpu.SMEM((8, 128), i32),
            pltpu.SMEM((16, 128), i32),
            dma((2,)),
            pltpu.VMEM((9, 5, ROWS, 128), i32),
            pltpu.VMEM((8, 128), f32),
            pltpu.VMEM((GZ - 1, 8, 128), f32),
            pltpu.VMEM((8, 128), f32),
            pltpu.VMEM((3, 8, 128), f32),
            dma((9,)),
            dma((9,)),
            dma((GZ - 1,)),
            dma((GZ - 1,)),
            dma((3,)),
            dma((3,)),
            pltpu.VMEM((8, 128), f32),
            pltpu.VMEM((3, 8, 128), f32),
            dma((3,)),
            dma((3,)),
            dma,
            pltpu.VMEM((2, CAP), jnp.int32),
            pltpu.VMEM((3, ROWS, 128), jnp.int32),
            dma((2,)),
        ],
        compiler_params=pltpu.CompilerParams(
            collective_id=0, has_side_effects=True, vmem_limit_bytes=VMEM_LIMIT
        ),
        name="exchange",
    )(
        pltpu.with_memory_space_constraint(eddy_cells.reshape(2, CAP), pltpu.HBM),
        pltpu.with_memory_space_constraint(eddy_signs.reshape(3, ROWS, 128), pltpu.HBM),
        eddy_counts,
        mean_flow,
    )
    return pl.pallas_call(
        evaluate,
        out_shape=jax.ShapeDtypeStruct((3, TY, TZ), f32),
        in_specs=[smem, vmem, vmem, vmem, vmem, vmem, vmem],
        out_specs=anywhere,
        scratch_shapes=[
            pltpu.VMEM((3, TY, TZ), f32),
            pltpu.VMEM((BLOCK, 3 * TZ), f32),
            pltpu.VMEM((8, TY), f32),
            dma((BLOCKS,)),
        ],
        compiler_params=pltpu.CompilerParams(vmem_limit_bytes=VMEM_LIMIT),
        name="evaluate",
    )(bounds, total, lists, stress_diag, stress_shear, own, held)


def solution(mesh):
    return jax.shard_map(
        body,
        mesh=mesh,
        in_specs=(
            P("gy", "gz", None, None),
            P("gy", "gz", None, None),
            P("gy", "gz"),
            P(None, "gy"),
            P(None, "gy"),
            P(None, "gy", "gz"),
        ),
        out_specs=P(None, "gy", "gz"),
        check_vma=False,
    )
```

time: 39.8 us -> 27.3 us (0.69)
  the two profiles are of different devices: /device:TPU:1 before, /device:TPU:32 now
where the time goes in v3:
time: 27.3 us
  Pallas kernels  26.6 us (97%)
  between operations  0.68 us (2%)
    pallas_call x1, Pallas kernels, body(): pl.pallas_call(exchange, out_shape=(pltpu.VMEM((9, 5, ROWS, 128), i32), j...  20.3 us
    pallas_call x1, Pallas kernels, body(): pl.pallas_call(evaluate, out_shape=jax.ShapeDtypeStruct((3, TY, TZ), f32)...  6.26 us

profile of v3, /device:TPU:32, one launch (start us, length us, event | category | flops | bytes accessed | tf_op | source)
XLA Modules:
  0.0 27.3 jit_solution(15786012250276786898)
XLA Ops:
  0.0 0.0 copy-start.1
  0.0 0.0 copy-start
  0.7 20.3 %exchange.1 = (s32[9,5,16,128]{3,2,1,0:T(8,128)S(1)}, s32[16,128]{1,0:T(8,128)S(1)}, f32[8,128]{1,0:T(8,128)S(1)}, f32[8,256,768]{2,1,0:T(8,128)S(1)}, f32[3,2048,256]{2,1,0:T(8,128)S(1)}) custom-call(s32[2,2048]{1,0:T(2,128)} %bitcast.3, s32[3,16,128]{2,1,0:T(8,128)} %bitcast.2, s32[1,1]{1,0:T(1,128)S(6)} %copy.7.count, f32[3,2048,256]{2,1,0:T(8,128)} %mean.1), custom_call_target="tpu_custom_call" | custom-call | tf_op jit(solution)/shard_map/exchange/pallas_call | solution.py:440
  21.0 0.0 copy-done.1
  21.0 0.0 copy-done
  21.0 6.3 %evaluate.1 = f32[3,2048,256]{2,1,0:T(8,128)} custom-call(s32[16,128]{1,0:T(8,128)S(1)} %get-tuple-element.10.bounds, f32[8,128]{1,0:T(8,128)S(1)} %get-tuple-element.11.total, s32[9,5,16,128]{3,2,1,0:T(8,128)S(1)} %get-tuple-element.12.lists, f32[3,2048]{1,0:T(4,128)S(1)} %copy-done, f32[3,2048]{1,0:T(4,128)S(1)} %copy-done.1, ...), custom_call_target="tpu_custom_call" | custom-call | tf_op jit(solution)/shard_map/evaluate/pallas_call | solution.py:488
Async XLA Ops:
  0.0 21.0 %copy-start.1 = (f32[3,2048]{1,0:T(4,128)S(1)}, f32[3,2048]{1,0:T(4,128)}, u32[]{:S(2)}) copy-start(f32[3,2048]{1,0:T(4,128)} %shear.1) | copy-start | bytes 73732
  0.0 21.0 %copy-start = (f32[3,2048]{1,0:T(4,128)S(1)}, f32[3,2048]{1,0:T(4,128)}, u32[]{:S(2)}) copy-start(f32[3,2048]{1,0:T(4,128)} %diag.1) | copy-start | bytes 73732

commit v4 on v3

--- a/solution.py
+++ b/solution.py
@@ -20,6 +20,8 @@
 OFFSETS = tuple((di, dj) for di in (-1, 0, 1) for dj in (-1, 0, 1))
 OWN = 4
 SPLIT = 8
+UNROLL_OWN = 2
+UNROLL_SIDE = 2
 OWN_CHUNKS = 5
 SIDE_CHUNKS = 3
 END_CHUNKS = 2
@@ -28,45 +30,66 @@
 def sort_keys(vregs):
     lane = lax.broadcasted_iota(jnp.int32, (8, 128), 1)
     row = lax.broadcasted_iota(jnp.int32, (8, 128), 0)
-    index = row * 128 + lane
-    bits = CAP.bit_length() - 1
-    for up in range(1, bits + 1):
+    flat = [half for halves in vregs for half in halves]
+    flat += [jnp.zeros((8, 128), jnp.int32)] * (16 - len(flat))
+    turned = jnp.concatenate(flat, axis=0).T
+    x = [turned[8 * i : 8 * i + 8, :] for i in range(16)]
+    zero = {t: (lax.shift_right_logical(row, t) & 1) == 0 for t in range(3)}
+    zero |= {t: (lax.shift_right_logical(lane, t - 7) & 1) == 0 for t in range(7, 11)}
+
+    def rising(up, i):
+        if up == 11:
+            return True
+        if 3 <= up < 7:
+            return not (i >> (up - 3)) & 1
+        return zero[up]
+
+    for up in range(1, 12):
         for step in range(up - 1, -1, -1):
-            if step == 10:
-                vregs = [
-                    (jnp.minimum(low, high), jnp.maximum(low, high)) for low, high in vregs
-                ]
-                continue
-            own_bit = lax.shift_right_logical(index, step) & 1
-            lower = own_bit == 0
-            axis, size, by = (1, 128, 1 << step) if step < 7 else (0, 8, 1 << (step - 7))
-            sorted_lists = []
-            for halves in vregs:
-                done = []
-                for half, x in enumerate(halves):
-                    if up < 10:
-                        take_min = ((lax.shift_right_logical(index, up) & 1) ^ own_bit) == 0
-                    elif up == 10 and half == 1:
-                        take_min = own_bit == 1
+            new = [None] * 16
+            if 3 <= step < 7:
+                for i in range(16):
+                    j = i ^ (1 << (step - 3))
+                    if j < i:
+                        continue
+                    low, high = jnp.minimum(x[i], x[j]), jnp.maximum(x[i], x[j])
+                    r = rising(up, i)
+                    if r is True:
+                        new[i], new[j] = low, high
+                    elif r is False:
+                        new[i], new[j] = high, low
                     else:
-                        take_min = lower
-                    ahead = pltpu.roll(x, size - by, axis)
+                        new[i], new[j] = jnp.where(r, low, high), jnp.where(r, high, low)
+            else:
+                axis, size, by = (0, 8, 1 << step) if step < 3 else (1, 128, 1 << (step - 7))
+                lower = zero[step]
+                same = None
+                for i in range(16):
+                    ahead = pltpu.roll(x[i], size - by, axis)
                     if 2 * by == size:
                         other = ahead
                     else:
-                        other = jnp.where(lower, ahead, pltpu.roll(x, by, axis))
-                    done.append(
-                        jnp.where(take_min, jnp.minimum(x, other), jnp.maximum(x, other))
-                    )
-                sorted_lists.append(tuple(done))
-            vregs = sorted_lists
-    return vregs
+                        other = jnp.where(lower, ahead, pltpu.roll(x[i], by, axis))
+                    low, high = jnp.minimum(x[i], other), jnp.maximum(x[i], other)
+                    r = rising(up, i)
+                    if r is True:
+                        new[i] = jnp.where(lower, low, high)
+                    elif r is False:
+                        new[i] = jnp.where(lower, high, low)
+                    else:
+                        same = lower == r if same is None else same
+                        new[i] = jnp.where(same, low, high)
+            x = new
+    back = jnp.concatenate(x, axis=0).T
+    return [(back[16 * i : 16 * i + 8, :], back[16 * i + 8 : 16 * i + 16, :]) for i in range(len(vregs))]
 
 
 def exchange(
     cells_in,
     signs_in,
     count,
+    diag_in,
+    shear_in,
     mean,
     lists,
     bounds,
@@ -98,10 +121,15 @@
     cells,
     signs,
     input_sem,
+    scales,
+    diag,
+    shear,
 ):
     inputs = [
         pltpu.make_async_copy(cells_in, cells, input_sem.at[0]),
         pltpu.make_async_copy(signs_in, signs, input_sem.at[1]),
+        pltpu.make_async_copy(diag_in, diag, input_sem.at[2]),
+        pltpu.make_async_copy(shear_in, shear, input_sem.at[3]),
     ]
     for copy in inputs:
         copy.start()
@@ -176,6 +204,7 @@
 
     for copy in inputs:
         copy.wait()
+    fill_scales(scales, diag, shear)
     for r in range(ROWS):
         for k in range(2):
             places[k, r : r + 1, :] = cells[k : k + 1, 128 * r : 128 * r + 128]
@@ -253,10 +282,9 @@
         number = jnp.maximum(own_bounds[0, BLOCKS + b] - begin, 0)
         own[b] = product(lists, 0, b, [0, begin, 0], [0, number, 0], 0, OWN_CHUNKS)
 
-    pl.loop(0, SPLIT)(own_block)
+    pl.loop(0, SPLIT, unroll=UNROLL_OWN)(own_block)
     end_phase(1, counting, part3)
     counting = start_phase(2)
-    pl.loop(SPLIT, BLOCKS)(own_block)
 
     bounds[OWN : OWN + 1, :] = own_edges[0:1, :]
 
@@ -298,17 +326,45 @@
             dj: product(lists, dj, b, *chunk_counts(list_bounds, dj, b), 0, SIDE_CHUNKS)
             for dj in (-1, 1)
         }
-        for c in range(3):
-            for half, dj in ((0, -1), (1, 1)):
-                at = c * TZ + half * HALF
-                own[b, :, at : at + HALF] += parts[dj][:, c * HALF : (c + 1) * HALF]
-
-    pl.loop(0, BLOCKS)(side_block)
+        k = stress(scales, b)
+        raw = [
+            jnp.concatenate(
+                [
+                    own[b, :, c * TZ + half * HALF : c * TZ + (half + 1) * HALF]
+                    + parts[dj][:, c * HALF : (c + 1) * HALF]
+                    for half, dj in ((0, -1), (1, 1))
+                ],
+                axis=1,
+            )
+            for c in range(3)
+        ]
+        for c, value in enumerate(transformed(k, raw)):
+            own[b, :, c * TZ : (c + 1) * TZ] = value
+
     for b in (0, BLOCKS - 1):
         ranges = chunk_counts(list_bounds, 0, b)
         own[b] += product(lists, 0, jnp.int32(b), *ranges, 0, END_CHUNKS)
+    pl.loop(0, BLOCKS, unroll=UNROLL_SIDE)(side_block)
     end_phase(2, counting, total)
     fetch.wait()
+
+
+def fill_scales(scales, diag, shear):
+    scales[0:3, :] = diag[...] * (1.5 / (HALF * HALF))
+    scales[3:6, :] = shear[...] * (1.5 / (HALF * HALF))
+    scales[6:8, :] = jnp.zeros((2, TY), jnp.float32)
+
+
+def stress(scales, b):
+    return scales[:, pl.ds(pl.multiple_of(b * BLOCK, BLOCK), BLOCK)].T
+
+
+def transformed(k, raw):
+    return (
+        k[:, 0:1] * raw[0],
+        k[:, 3:4] * raw[0] + k[:, 1:2] * raw[1],
+        k[:, 4:5] * raw[0] + k[:, 5:6] * raw[1] + k[:, 2:3] * raw[2],
+    )
 
 
 def chunk_counts(bounds, dj, b):
@@ -372,20 +428,12 @@
         rows = pl.ds(pl.multiple_of(b * BLOCK, BLOCK), BLOCK)
         return pltpu.make_async_copy(buffer.at[:, rows, :], out.at[:, rows, :], out_sem.at[b])
 
-    gain = jnp.sqrt(TY * GY * (TZ * GZ) / (HALF * HALF) / total[0:1, 0:1]) * (1.5 / (HALF * HALF))
-    scales[0:3, :] = diag[...] * gain
-    scales[3:6, :] = shear[...] * gain
-    scales[6:8, :] = jnp.zeros((2, TY), jnp.float32)
-
-    def finish(b, raw):
+    gain = jnp.sqrt(TY * GY * (TZ * GZ) / (HALF * HALF) / total[0:1, 0:1])
+
+    def finish(b, field):
         rows = pl.ds(pl.multiple_of(b * BLOCK, BLOCK), BLOCK)
-        k = scales[:, rows].T
-        raw = [raw[:, c * TZ : (c + 1) * TZ] for c in range(3)]
-        buffer[0, rows, :] = mean[0, rows, :] + k[:, 0:1] * raw[0]
-        buffer[1, rows, :] = mean[1, rows, :] + k[:, 3:4] * raw[0] + k[:, 1:2] * raw[1]
-        buffer[2, rows, :] = (
-            mean[2, rows, :] + k[:, 4:5] * raw[0] + k[:, 5:6] * raw[1] + k[:, 2:3] * raw[2]
-        )
+        for c in range(3):
+            buffer[c, rows, :] = mean[c, rows, :] + gain * field[:, c * TZ : (c + 1) * TZ]
         save(b).start()
 
     def leftovers(b):
@@ -406,7 +454,7 @@
 
         @pl.when(some)
         def _():
-            acc[...] = own[b]
+            acc[...] = jnp.zeros_like(acc)
             for count, (dj, begins, numbers, done) in zip(counts, jobs):
 
                 def more(step, carry, dj=dj, begins=begins, numbers=numbers, done=done):
@@ -420,6 +468,10 @@
                     return carry
 
                 lax.fori_loop(0, jnp.maximum(count - done + 1, 0) // 2, more, 0)
+            fill_scales(scales, diag, shear)
+            raw = [acc[:, c * TZ : (c + 1) * TZ] for c in range(3)]
+            for c, value in enumerate(transformed(stress(scales, b), raw)):
+                acc[:, c * TZ : (c + 1) * TZ] = own[b, :, c * TZ : (c + 1) * TZ] + value
             finish(b, acc)
 
         @pl.when(jnp.logical_not(some))
@@ -446,7 +498,7 @@
             pltpu.VMEM((BLOCKS, BLOCK, 3 * TZ), f32),
             pltpu.VMEM((3, TY, TZ), f32),
         ),
-        in_specs=[hbm, hbm, smem, hbm],
+        in_specs=[hbm, hbm, smem, hbm, hbm, hbm],
         out_specs=(vmem, vmem, vmem, vmem, vmem),
         scratch_shapes=[
             pltpu.VMEM((2, ROWS, 128), jnp.int32),
@@ -473,7 +525,10 @@
             dma,
             pltpu.VMEM((2, CAP), jnp.int32),
             pltpu.VMEM((3, ROWS, 128), jnp.int32),
-            dma((2,)),
+            dma((4,)),
+            pltpu.VMEM((8, TY), f32),
+            pltpu.VMEM((3, TY), f32),
+            pltpu.VMEM((3, TY), f32),
         ],
         compiler_params=pltpu.CompilerParams(
             collective_id=0, has_side_effects=True, vmem_limit_bytes=VMEM_LIMIT
@@ -483,6 +538,8 @@
         pltpu.with_memory_space_constraint(eddy_cells.reshape(2, CAP), pltpu.HBM),
         pltpu.with_memory_space_constraint(eddy_signs.reshape(3, ROWS, 128), pltpu.HBM),
         eddy_counts,
+        pltpu.with_memory_space_constraint(stress_diag, pltpu.HBM),
+        pltpu.with_memory_space_constraint(stress_shear, pltpu.HBM),
         mean_flow,
     )
     return pl.pallas_call(

time: 27.3 us -> 24.1 us (0.88)
  the two profiles are of different devices: /device:TPU:32 before, /device:TPU:1 now
where the time goes in v4:
time: 24.1 us
  Pallas kernels  23.4 us (97%)
  between operations  0.68 us (3%)
    pallas_call x1, Pallas kernels, body(): pl.pallas_call(exchange, out_shape=(pltpu.VMEM((9, 5, ROWS, 128), i32), j...  19.5 us
    pallas_call x1, Pallas kernels, body(): pl.pallas_call(evaluate, out_shape=jax.ShapeDtypeStruct((3, TY, TZ), f32)...  3.88 us

profile of v4, /device:TPU:1, one launch (start us, length us, event | category | flops | bytes accessed | tf_op | source)
XLA Modules:
  0.0 24.1 jit_solution(17954723884160466523)
XLA Ops:
  0.0 0.0 copy-start.1
  0.0 0.0 copy-start
  0.7 19.5 %exchange.1 = (s32[9,5,16,128]{3,2,1,0:T(8,128)S(1)}, s32[16,128]{1,0:T(8,128)S(1)}, f32[8,128]{1,0:T(8,128)S(1)}, f32[8,256,768]{2,1,0:T(8,128)S(1)}, f32[3,2048,256]{2,1,0:T(8,128)S(1)}) custom-call(s32[2,2048]{1,0:T(2,128)} %bitcast.3, s32[3,16,128]{2,1,0:T(8,128)} %bitcast.2, s32[1,1]{1,0:T(1,128)S(6)} %copy.7.count, f32[3,2048]{1,0:T(4,128)} %diag.1, ...), custom_call_target="tpu_custom_call" | custom-call | tf_op jit(solution)/shard_map/exchange/pallas_call | solution.py:492
  20.2 0.0 copy-done.1
  20.2 0.0 copy-done
  20.2 3.9 %evaluate.1 = f32[3,2048,256]{2,1,0:T(8,128)} custom-call(s32[16,128]{1,0:T(8,128)S(1)} %get-tuple-element.10.bounds, f32[8,128]{1,0:T(8,128)S(1)} %get-tuple-element.11.total, s32[9,5,16,128]{3,2,1,0:T(8,128)S(1)} %get-tuple-element.12.lists, f32[3,2048]{1,0:T(4,128)S(1)} %copy-done, f32[3,2048]{1,0:T(4,128)S(1)} %copy-done.1, ...), custom_call_target="tpu_custom_call" | custom-call | tf_op jit(solution)/shard_map/evaluate/pallas_call | solution.py:545
Async XLA Ops:
  0.0 20.2 %copy-start.1 = (f32[3,2048]{1,0:T(4,128)S(1)}, f32[3,2048]{1,0:T(4,128)}, u32[]{:S(2)}) copy-start(f32[3,2048]{1,0:T(4,128)} %shear.1) | copy-start | bytes 73732
  0.0 20.2 %copy-start = (f32[3,2048]{1,0:T(4,128)S(1)}, f32[3,2048]{1,0:T(4,128)}, u32[]{:S(2)}) copy-start(f32[3,2048]{1,0:T(4,128)} %diag.1) | copy-start | bytes 73732

commit v5 on v4

--- a/solution.py
+++ b/solution.py
@@ -22,8 +22,8 @@
 SPLIT = 8
 UNROLL_OWN = 2
 UNROLL_SIDE = 2
-OWN_CHUNKS = 5
-SIDE_CHUNKS = 3
+OWN_CHUNKS = 6
+SIDE_CHUNKS = 4
 END_CHUNKS = 2
 
 
@@ -146,9 +146,9 @@
         return (gy - lax.rem(gy, 4) + lax.rem(gy + d, 4), gz)
 
     groups = [
+        [at(4 * d, 0) for d in range(1, 4)],
+        [along_y(d) for d in range(1, 4)],
         [at(0, d) for d in range(1, GZ)],
-        [along_y(d) for d in range(1, 4)],
-        [at(4 * d, 0) for d in range(1, 4)],
     ]
     for group in groups:
         for partner in group:
@@ -273,8 +273,6 @@
     lists[OWN] = stage[0]
     to_scalars = pltpu.make_async_copy(own_edges, own_bounds, bound_sem.at[0])
     to_scalars.start()
-    end_phase(0, counting, part2)
-    counting = start_phase(1)
     to_scalars.wait()
 
     def own_block(b):
@@ -282,7 +280,10 @@
         number = jnp.maximum(own_bounds[0, BLOCKS + b] - begin, 0)
         own[b] = product(lists, 0, b, [0, begin, 0], [0, number, 0], 0, OWN_CHUNKS)
 
-    pl.loop(0, SPLIT, unroll=UNROLL_OWN)(own_block)
+    pl.loop(0, 2, unroll=UNROLL_OWN)(own_block)
+    end_phase(0, counting, part2)
+    counting = start_phase(1)
+    pl.loop(2, 8, unroll=UNROLL_OWN)(own_block)
     end_phase(1, counting, part3)
     counting = start_phase(2)
 
@@ -316,7 +317,17 @@
                 lists[slot] = jnp.zeros((5, ROWS, 128), jnp.int32)
                 bounds[slot : slot + 1, :] = jnp.zeros((1, 128), jnp.int32)
 
-    bounds[9:16, :] = jnp.zeros((7, 128), jnp.int32)
+    every = [bounds[slot : slot + 1, :] for slot in range(9)]
+    number = [jnp.maximum(pltpu.roll(row, 128 - BLOCKS, 1) - row, 0) for row in every]
+    over = [
+        number[OWN] - OWN_CHUNKS,
+        number[1] + number[7] - END_CHUNKS,
+        number[0] + number[3] + number[6] - SIDE_CHUNKS,
+        number[2] + number[5] + number[8] - SIDE_CHUNKS,
+    ]
+    most = jnp.maximum(jnp.maximum(over[0], over[1]), jnp.maximum(over[2], over[3]))
+    most = jnp.max(jnp.where(lane16[0:1, :] < BLOCKS, most, 0), axis=1, keepdims=True)
+    bounds[9:16, :] = jnp.broadcast_to(most, (7, 128))
     to_scalars = pltpu.make_async_copy(bounds, list_bounds, bound_sem.at[1])
     to_scalars.start()
     to_scalars.wait()
@@ -444,39 +455,48 @@
             jobs.append((dj, *chunk_counts(bounds, dj, b), done))
         return jobs
 
-    @pl.loop(0, BLOCKS)
-    def _(b):
-        jobs = leftovers(b)
-        counts = [numbers[0] + numbers[1] + numbers[2] for _, _, numbers, _ in jobs]
-        some = counts[0] > jobs[0][3]
-        for count, job in zip(counts[1:], jobs[1:]):
-            some = jnp.logical_or(some, count > job[3])
-
-        @pl.when(some)
-        def _():
-            acc[...] = jnp.zeros_like(acc)
-            for count, (dj, begins, numbers, done) in zip(counts, jobs):
-
-                def more(step, carry, dj=dj, begins=begins, numbers=numbers, done=done):
-                    extra = product(lists, dj, b, begins, numbers, done + step * 2, 2)
-                    if dj == 0:
-                        acc[...] += extra
-                    else:
-                        for c in range(3):
-                            at = c * TZ + (0 if dj < 0 else HALF)
-                            acc[:, at : at + HALF] += extra[:, c * HALF : (c + 1) * HALF]
-                    return carry
-
-                lax.fori_loop(0, jnp.maximum(count - done + 1, 0) // 2, more, 0)
-            fill_scales(scales, diag, shear)
-            raw = [acc[:, c * TZ : (c + 1) * TZ] for c in range(3)]
-            for c, value in enumerate(transformed(stress(scales, b), raw)):
-                acc[:, c * TZ : (c + 1) * TZ] = own[b, :, c * TZ : (c + 1) * TZ] + value
-            finish(b, acc)
-
-        @pl.when(jnp.logical_not(some))
-        def _():
+    leftover = bounds[9, 0]
+
+    @pl.when(leftover == 0)
+    def _():
+        for b in range(BLOCKS):
             finish(b, own.at[b])
+
+    @pl.when(leftover > 0)
+    def _():
+        @pl.loop(0, BLOCKS)
+        def _(b):
+            jobs = leftovers(b)
+            counts = [numbers[0] + numbers[1] + numbers[2] for _, _, numbers, _ in jobs]
+            some = counts[0] > jobs[0][3]
+            for count, job in zip(counts[1:], jobs[1:]):
+                some = jnp.logical_or(some, count > job[3])
+
+            @pl.when(some)
+            def _():
+                acc[...] = jnp.zeros_like(acc)
+                for count, (dj, begins, numbers, done) in zip(counts, jobs):
+
+                    def more(step, carry, dj=dj, begins=begins, numbers=numbers, done=done):
+                        extra = product(lists, dj, b, begins, numbers, done + step * 2, 2)
+                        if dj == 0:
+                            acc[...] += extra
+                        else:
+                            for c in range(3):
+                                at = c * TZ + (0 if dj < 0 else HALF)
+                                acc[:, at : at + HALF] += extra[:, c * HALF : (c + 1) * HALF]
+                        return carry
+
+                    lax.fori_loop(0, jnp.maximum(count - done + 1, 0) // 2, more, 0)
+                fill_scales(scales, diag, shear)
+                raw = [acc[:, c * TZ : (c + 1) * TZ] for c in range(3)]
+                for c, value in enumerate(transformed(stress(scales, b), raw)):
+                    acc[:, c * TZ : (c + 1) * TZ] = own[b, :, c * TZ : (c + 1) * TZ] + value
+                finish(b, acc)
+
+            @pl.when(jnp.logical_not(some))
+            def _():
+                finish(b, own.at[b])
 
     for b in range(BLOCKS):
         save(b).wait()
@@ -509,19 +529,19 @@
             dma((2,)),
             pltpu.VMEM((9, 5, ROWS, 128), i32),
             pltpu.VMEM((8, 128), f32),
-            pltpu.VMEM((GZ - 1, 8, 128), f32),
+            pltpu.VMEM((3, 8, 128), f32),
             pltpu.VMEM((8, 128), f32),
             pltpu.VMEM((3, 8, 128), f32),
             dma((9,)),
             dma((9,)),
-            dma((GZ - 1,)),
-            dma((GZ - 1,)),
+            dma((3,)),
+            dma((3,)),
             dma((3,)),
             dma((3,)),
             pltpu.VMEM((8, 128), f32),
-            pltpu.VMEM((3, 8, 128), f32),
-            dma((3,)),
-            dma((3,)),
+            pltpu.VMEM((GZ - 1, 8, 128), f32),
+            dma((GZ - 1,)),
+            dma((GZ - 1,)),
             dma,
             pltpu.VMEM((2, CAP), jnp.int32),
             pltpu.VMEM((3, ROWS, 128), jnp.int32),

time: 24.1 us -> 24.2 us (level); the launches traced: 24.1 us -> 23.8 us
  Pallas kernels: 23.4 us -> 23.1 us
    pallas_call x1, Pallas kernels: 3.88 us -> 3.56 us  [body(): pl.pallas_call(evaluate, out_shape=jax.ShapeDtypeStruct((3, TY, TZ), f32)...]
where the time goes in v5:
time: 24.2 us; the launch traced here: 23.8 us
  Pallas kernels  23.1 us (95%)
  between operations  0.68 us (3%)
    pallas_call x1, Pallas kernels, body(): pl.pallas_call(exchange, out_shape=(pltpu.VMEM((9, 5, ROWS, 128), i32), j...  19.5 us
    pallas_call x1, Pallas kernels, body(): pl.pallas_call(evaluate, out_shape=jax.ShapeDtypeStruct((3, TY, TZ), f32)...  3.56 us

profile of v5, /device:TPU:1, one launch (start us, length us, event | category | flops | bytes accessed | tf_op | source)
XLA Modules:
  0.0 23.8 jit_solution(6557228793407876237)
XLA Ops:
  0.0 0.0 copy-start.1
  0.0 0.0 copy-start
  0.7 19.5 %exchange.1 = (s32[9,5,16,128]{3,2,1,0:T(8,128)S(1)}, s32[16,128]{1,0:T(8,128)S(1)}, f32[8,128]{1,0:T(8,128)S(1)}, f32[8,256,768]{2,1,0:T(8,128)S(1)}, f32[3,2048,256]{2,1,0:T(8,128)S(1)}) custom-call(s32[2,2048]{1,0:T(2,128)} %bitcast.3, s32[3,16,128]{2,1,0:T(8,128)} %bitcast.2, s32[1,1]{1,0:T(1,128)S(6)} %copy.7.count, f32[3,2048]{1,0:T(4,128)} %diag.1, ...), custom_call_target="tpu_custom_call" | custom-call | tf_op jit(solution)/shard_map/exchange/pallas_call | solution.py:512
  20.2 0.0 copy-done.1
  20.2 0.0 copy-done
  20.2 3.6 %evaluate.1 = f32[3,2048,256]{2,1,0:T(8,128)} custom-call(s32[16,128]{1,0:T(8,128)S(1)} %get-tuple-element.10.bounds, f32[8,128]{1,0:T(8,128)S(1)} %get-tuple-element.11.total, s32[9,5,16,128]{3,2,1,0:T(8,128)S(1)} %get-tuple-element.12.lists, f32[3,2048]{1,0:T(4,128)S(1)} %copy-done, f32[3,2048]{1,0:T(4,128)S(1)} %copy-done.1, ...), custom_call_target="tpu_custom_call" | custom-call | tf_op jit(solution)/shard_map/evaluate/pallas_call | solution.py:565
Async XLA Ops:
  0.0 20.2 %copy-start.1 = (f32[3,2048]{1,0:T(4,128)S(1)}, f32[3,2048]{1,0:T(4,128)}, u32[]{:S(2)}) copy-start(f32[3,2048]{1,0:T(4,128)} %shear.1) | copy-start | bytes 73732
  0.0 20.2 %copy-start = (f32[3,2048]{1,0:T(4,128)S(1)}, f32[3,2048]{1,0:T(4,128)}, u32[]{:S(2)}) copy-start(f32[3,2048]{1,0:T(4,128)} %diag.1) | copy-start | bytes 73732

commit v6 on v5

--- a/solution.py
+++ b/solution.py
@@ -21,7 +21,7 @@
 OWN = 4
 SPLIT = 8
 UNROLL_OWN = 2
-UNROLL_SIDE = 2
+UNROLL_SIDE = 4
 OWN_CHUNKS = 6
 SIDE_CHUNKS = 4
 END_CHUNKS = 2

time: 24.2 us -> 24.1 us (level)
  no operation moved by 1% of the time
where the time goes in v6:
time: 24.1 us; the launch traced here: 23.7 us
  Pallas kernels  23 us (95%)
  between operations  0.68 us (3%)
    pallas_call x1, Pallas kernels, body(): pl.pallas_call(exchange, out_shape=(pltpu.VMEM((9, 5, ROWS, 128), i32), j...  19.4 us
    pallas_call x1, Pallas kernels, body(): pl.pallas_call(evaluate, out_shape=jax.ShapeDtypeStruct((3, TY, TZ), f32)...  3.56 us

profile of v6, /device:TPU:1, one launch (start us, length us, event | category | flops | bytes accessed | tf_op | source)
XLA Modules:
  0.0 23.7 jit_solution(1974823183448304387)
XLA Ops:
  0.0 0.0 copy-start.1
  0.0 0.0 copy-start
  0.7 19.4 %exchange.1 = (s32[9,5,16,128]{3,2,1,0:T(8,128)S(1)}, s32[16,128]{1,0:T(8,128)S(1)}, f32[8,128]{1,0:T(8,128)S(1)}, f32[8,256,768]{2,1,0:T(8,128)S(1)}, f32[3,2048,256]{2,1,0:T(8,128)S(1)}) custom-call(s32[2,2048]{1,0:T(2,128)} %bitcast.3, s32[3,16,128]{2,1,0:T(8,128)} %bitcast.2, s32[1,1]{1,0:T(1,128)S(6)} %copy.7.count, f32[3,2048]{1,0:T(4,128)} %diag.1, ...), custom_call_target="tpu_custom_call" | custom-call | tf_op jit(solution)/shard_map/exchange/pallas_call | solution.py:512
  20.1 0.0 copy-done.1
  20.1 0.0 copy-done
  20.1 3.6 %evaluate.1 = f32[3,2048,256]{2,1,0:T(8,128)} custom-call(s32[16,128]{1,0:T(8,128)S(1)} %get-tuple-element.10.bounds, f32[8,128]{1,0:T(8,128)S(1)} %get-tuple-element.11.total, s32[9,5,16,128]{3,2,1,0:T(8,128)S(1)} %get-tuple-element.12.lists, f32[3,2048]{1,0:T(4,128)S(1)} %copy-done, f32[3,2048]{1,0:T(4,128)S(1)} %copy-done.1, ...), custom_call_target="tpu_custom_call" | custom-call | tf_op jit(solution)/shard_map/evaluate/pallas_call | solution.py:565
Async XLA Ops:
  0.0 20.1 %copy-start.1 = (f32[3,2048]{1,0:T(4,128)S(1)}, f32[3,2048]{1,0:T(4,128)}, u32[]{:S(2)}) copy-start(f32[3,2048]{1,0:T(4,128)} %shear.1) | copy-start | bytes 73732
  0.0 20.1 %copy-start = (f32[3,2048]{1,0:T(4,128)S(1)}, f32[3,2048]{1,0:T(4,128)}, u32[]{:S(2)}) copy-start(f32[3,2048]{1,0:T(4,128)} %diag.1) | copy-start | bytes 73732
